TPU v7x, 32 devices: a whole 2x2x4 slice. The times are simulated.
32 devices in a mesh: section: 4 (over z), seq: 8 (over y, x, core).
Axes of the slice: x: 2, y: 2, z: 4, core: 2. Of those that a mesh axis runs over, the one named last changes fastest.
Arguments:
- input_in_transit: bfloat16 [4, 1024, 4096], P('section', 'seq'), may hold values from -6 to 6
- mixer_norm_gain: float32 [4, 4096], P('section'), may hold values from 0.5 to 1.5
- convolution_weight: float32 [4, 4, 4096], P('section'), may hold values from -3 to 3
- convolution_bias: float32 [4, 4096], P('section'), may hold values from -2 to 2
- input_projection: bfloat16 [4, 4096, 288], P('section', 'seq'), may hold values from -0.09375 to 0.09375
- step_size_projection: bfloat16 [4, 256, 4096], P('section', None, 'seq'), may hold values from -0.375 to 0.375
- step_size_bias: float32 [4, 4096], P('section'), may hold values from -6.9 to -2.3
- log_decay_rates: float32 [4, 4096, 16], P('section'), may hold values from 0 to 2.77
- mixer_skip_weight: float32 [4, 4096], P('section'), may hold values from 0.5 to 1.5
- expert_norm_gain: float32 [4, 4096], P('section'), may hold values from 0.1 to 1.9
- router: bfloat16 [4, 4096, 16], P('section'), may hold values from -0.09375 to 0.09375
- gate_weight: bfloat16 [4, 4096, 12288], P('section', None, 'seq'), may hold values from -0.09375 to 0.09375
- up_weight: bfloat16 [4, 4096, 12288], P('section', None, 'seq'), may hold values from -0.09375 to 0.09375
- down_weight: bfloat16 [4, 12288, 4096], P('section', 'seq'), may hold values from -0.0546875 to 0.0546875
- expert_index_table: int32 [2, 4, 1024, 2], P(None, 'section', 'seq'), may hold values from 0 to 15, as said below
Outputs:
- layer_out: bfloat16 [4, 1024, 4096], P('section', 'seq')
Inputs may be any that keep to these rules, and one draw needn't show every extreme that they name: `expert_index_table`: each token names two different experts of the 16; for each step and section, expert 0 is named by at most 8 tokens of any one block of 128 tokens.
All inputs are finite; a program needn't handle non-finite values.
Results may differ from a plain program's by a relative error of at most 0.0086.
Values may be sent and summed in bfloat16 or wider, within the bound.
A program may use at most 128 MiB of HBM per device.

v0:
```python
import jax
import jax.numpy as jnp
from jax import lax
from jax.sharding import PartitionSpec as P

STEPS = 2


def from_behind(block, axis, distance):
    devices = range(lax.axis_size(axis))
    route = [(i - distance, i) for i in devices if i - distance in devices]
    return lax.ppermute(block, axis, route)


def entering_2(x, axis, combine, identity):
    length, position = (lax.axis_size(axis), lax.axis_index(axis))
    everything = jax.tree.map(
        lambda part, kind: lax.all_gather(part.astype(kind), axis), x, (jnp.bfloat16, jnp.bfloat16)
    )
    start = jax.tree.map(
        lambda part, zero: jnp.broadcast_to(jnp.asarray(zero, part.dtype), part.shape), x, identity
    )

    def hop(k, before):
        reached = k < position
        new = combine(
            before, jax.tree.map(lambda part, own: part[k].astype(own.dtype), everything, x)
        )
        return jax.tree.map(lambda a, b: jnp.where(reached, a, b), new, before)

    return lax.fori_loop(0, length, hop, start)


def passed_along(x, axis, by):
    length = lax.axis_size(axis)
    return lax.ppermute(x, axis, [(i, (i + by) % length) for i in range(length)])


def rms_scale(values, gain):
    as_float = values.astype(jnp.float32)
    return (
        as_float * lax.rsqrt(jnp.mean(as_float * as_float, axis=-1, keepdims=True) + 1e-06) * gain
    )


def chain_step(earlier, later):
    return (earlier[0] * later[0], later[0] * earlier[1] + later[1])


def body(
    input_in_transit,
    mixer_norm_gain,
    convolution_weight,
    convolution_bias,
    input_projection,
    step_size_projection,
    step_size_bias,
    log_decay_rates,
    mixer_skip_weight,
    expert_norm_gain,
    router,
    gate_weight,
    up_weight,
    down_weight,
    expert_index_table,
):
    experts = router.shape[2]
    count_of_rows = input_in_transit.shape[1]
    width_of_model = input_in_transit.shape[2]
    nstate = log_decay_rates.shape[2]
    rank = step_size_projection.shape[1]
    kernel = convolution_weight.shape[1]
    capacity = count_of_rows // 16
    decay_rates = -jnp.exp(log_decay_rates[0]).T
    blocks = count_of_rows // 8
    own_gate = gate_weight[0]
    own_up = up_weight[0]
    own_down = down_weight[0]
    params = (input_projection[0], step_size_projection[0])
    present_value = input_in_transit[0]
    produced = present_value
    for step in range(STEPS):
        params = (
            lax.all_gather(input_projection[0], "seq", axis=0, tiled=True),
            lax.all_gather(step_size_projection[0], "seq", axis=1, tiled=True),
        )
        proj_full, step_full = params
        normed = rms_scale(present_value, mixer_norm_gain[0]).astype(jnp.bfloat16)
        rim_rows = from_behind(normed[count_of_rows - (kernel - 1) :], "seq", 1)
        padded = jnp.concatenate([rim_rows, normed], 0)
        convolved = convolution_bias[0]
        for tap in range(kernel):
            convolved = convolved + convolution_weight[0, tap] * padded[
                tap : tap + count_of_rows
            ].astype(jnp.float32)
        inner = jax.nn.silu(convolved)
        inner_b = inner.astype(jnp.bfloat16)
        projected = jnp.dot(inner_b, proj_full, preferred_element_type=jnp.float32)
        low_rank = projected[:, :rank].astype(jnp.bfloat16)
        b_in = projected[:, rank : rank + nstate]
        c_out = projected[:, rank + nstate :]
        step_size = jax.nn.softplus(
            jnp.dot(low_rank, step_full, preferred_element_type=jnp.float32) + step_size_bias[0]
        )
        cum_steps = jnp.cumsum(step_size, axis=0)
        blocked = (
            step_size.reshape(blocks, 8, width_of_model),
            inner.reshape(blocks, 8, width_of_model),
            b_in.reshape(blocks, 8, nstate),
            c_out.reshape(blocks, 8, nstate),
        )

        def first_pass(state, block):
            outputs = []
            for offset in range(8):
                factor = jnp.exp(block[0][offset][None, :] * decay_rates)
                state = (
                    factor * state
                    + block[2][offset][:, None] * (block[0][offset] * block[1][offset])[None, :]
                )
                outputs.append(jnp.sum(state * block[3][offset][:, None], axis=0))
            return (state, jnp.stack(outputs, 0))

        zeros_state = jnp.zeros((nstate, width_of_model), jnp.float32)
        ones_state = jnp.ones((nstate, width_of_model), jnp.float32)
        ending, local_out = lax.scan(first_pass, zeros_state, blocked)
        total_decay = jnp.exp(decay_rates * cum_steps[count_of_rows - 1][None, :])
        carried = entering_2((total_decay, ending), "seq", chain_step, (ones_state, zeros_state))
        entering = carried[1]

        def correction(block):
            steps_block, c_block = block
            decayed = jnp.exp(steps_block[:, None, :] * decay_rates[None, :, :])
            return jnp.sum(decayed * entering[None, :, :] * c_block[:, :, None], axis=1)

        corrected = lax.map(correction, (cum_steps.reshape(blocks, 8, width_of_model), blocked[3]))
        scanned = (local_out + corrected).reshape(count_of_rows, width_of_model)
        mixed_rows = (
            present_value.astype(jnp.float32) + (scanned + mixer_skip_weight[0] * inner)
        ).astype(jnp.bfloat16)
        chosen_ids = expert_index_table[step, 0]
        moe_in = rms_scale(mixed_rows, expert_norm_gain[0]).astype(jnp.bfloat16)
        logits = jnp.dot(moe_in, router[0], preferred_element_type=jnp.float32)
        one_hot = (
            chosen_ids[:, :, None] == jnp.arange(experts, dtype=jnp.int32)[None, None, :]
        ).astype(jnp.float32)
        first = jnp.sum(logits * one_hot[:, 0], axis=1)
        second = jnp.sum(logits * one_hot[:, 1], axis=1)
        weight_one = jax.nn.sigmoid(first - second)
        weight_two = 1.0 - weight_one
        route_weight = jnp.where(
            chosen_ids[:, 0] == 0,
            weight_one,
            jnp.where(chosen_ids[:, 1] == 0, weight_two, jnp.zeros_like(weight_one)),
        )
        routed = (chosen_ids[:, 0] == 0) | (chosen_ids[:, 1] == 0)
        routed_int = routed.astype(jnp.int32)
        slot = jnp.cumsum(routed_int) - routed_int
        dispatch = (
            (jnp.arange(capacity, dtype=jnp.int32)[:, None] == slot[None, :]) & routed[None, :]
        ).astype(jnp.bfloat16)
        sectioned = jnp.dot(dispatch, moe_in, preferred_element_type=jnp.float32).astype(
            jnp.bfloat16
        )
        gathered = lax.all_gather(sectioned, "seq", axis=0, tiled=True)
        gate_part = jnp.dot(gathered, own_gate, preferred_element_type=jnp.float32)
        up_part = jnp.dot(gathered, own_up, preferred_element_type=jnp.float32)
        hidden = (jax.nn.silu(gate_part) * up_part).astype(jnp.bfloat16)
        terms = jnp.dot(hidden, own_down, preferred_element_type=jnp.float32)
        summed = lax.psum_scatter(
            terms.astype(jnp.bfloat16), "seq", scatter_dimension=0, tiled=True
        )
        picked = jnp.einsum("cl,cd->ld", dispatch, summed, preferred_element_type=jnp.float32)
        combined = route_weight[:, None] * picked
        produced = (mixed_rows.astype(jnp.float32) + combined).astype(jnp.bfloat16)
        if step + 1 < STEPS:
            present_value = passed_along(produced, "section", 1)
    return produced[None]


def solution(mesh):
    return jax.shard_map(
        body,
        mesh=mesh,
        in_specs=(
            P("section", "seq", None),
            P("section", None),
            P("section", None, None),
            P("section", None),
            P("section", "seq", None),
            P("section", None, "seq"),
            P("section", None),
            P("section", None, None),
            P("section", None),
            P("section", None),
            P("section", None, None),
            P("section", None, "seq"),
            P("section", None, "seq"),
            P("section", "seq", None),
            P(None, "section", "seq", None),
        ),
        out_specs=P("section", "seq", None),
        check_vma=False,
    )
```

profile of v0, /device:TPU:1, one launch (start us, length us, event | category | flops | bytes accessed | tf_op | source)
XLA Modules:
  0.0 699.6 jit_solution(5574797647500048569)
XLA Ops:
  10.7 4.5 collective-permute-start
  16.2 3.4 divide_multiply_fusion.1
  19.7 21.3 %all-gather.13.cloned.1.call-done = bf16[1,4096,288]{1,2,0:T(8,128)(2,1)} async-done(((bf16[1,512,288]{1,2,0:T(8,128)(2,1)}), bf16[1,4096,288]{1,2,0:T(8,128)(2,1)}) %all-gather.13.cloned.1.call-update) | async-done | bytes 2359312 | tf_op jit(solution)/shard_map/all_gather | solution.py:84
  41.0 2.4 fusion.29
  44.9 26.1 %all-gather.15.cloned.1.call-done = bf16[1,256,4096]{2,1,0:T(8,128)(2,1)} async-done(((bf16[1,256,512]{2,1,0:T(8,128)(2,1)}), bf16[1,256,4096]{2,1,0:T(8,128)(2,1)}) %all-gather.15.cloned.1.call-update) | async-done | bytes 2097168 | tf_op jit(solution)/shard_map/all_gather | solution.py:85
  71.0 4.4 compare_select_fusion.1
  77.0 120.2 %while.76 = (s32[]{:T(128)}, f32[16,4096]{1,0:T(8,128)S(1)}, f32[16,8,4096]{2,1,0:T(8,128)}, f32[16,8,4096]{2,1,0:T(8,128)}, f32[16,4096]{1,0:T(8,128)S(1)}, /*i...) while((s32[]{:T(128)}, f32[16,4096]{1,0:T(8,128)S(1)}, ...), condition=%wide.region_10.11_spmd.clone, body=%wide.region_1.10_spmd.clone.sunk | while | flops 4587530 | bytes 5152236 | solution.py:126
  77.0 1.8 constant_dynamic-slice_fusion.41
  84.4 1.8 constant_dynamic-slice_fusion.41
  91.8 1.8 constant_dynamic-slice_fusion.41
  99.2 2.1 constant_dynamic-slice_fusion.41
  106.9 2.3 constant_dynamic-slice_fusion.41
  114.8 1.8 constant_dynamic-slice_fusion.41
  122.2 1.8 constant_dynamic-slice_fusion.41
  136.9 2.0 constant_dynamic-slice_fusion.41
  144.6 1.8 constant_dynamic-slice_fusion.41
  152.0 2.0 constant_dynamic-slice_fusion.41
  159.7 1.8 constant_dynamic-slice_fusion.41
  167.0 2.0 constant_dynamic-slice_fusion.41
  174.7 1.7 constant_dynamic-slice_fusion.41
  182.1 2.1 constant_dynamic-slice_fusion.41
  189.8 1.8 constant_dynamic-slice_fusion.41
  197.9 4.7 reduce_window_sum.26
  206.4 15.0 %all-gather.19.cloned.1.call-done = bf16[128,4096]{1,0:T(8,128)(2,1)} async-done(((bf16[16,4096]{1,0:T(8,128)(2,1)}), bf16[128,4096]{1,0:T(8,128)(2,1)}) %all-gather.19.cloned.1.call-update) | async-done | bytes 1048592 | tf_op jit(solution)/shard_map/all_gather | solution.py:18
  221.4 25.1 %all-gather.17.cloned.1.call-done = bf16[128,4096]{1,0:T(8,128)(2,1)} async-done(((bf16[16,4096]{1,0:T(8,128)(2,1)}), bf16[128,4096]{1,0:T(8,128)(2,1)}) %all-gather.17.cloned.1.call-update) | async-done | bytes 1048592 | tf_op jit(solution)/shard_map/all_gather | solution.py:18
  246.5 9.6 %while.77 = (s32[]{:T(128)}, f32[16,4096]{1,0:T(8,128)S(1)}, s32[]{:T(128)}, bf16[8,16,4096]{2,1,0:T(8,128)(2,1)}, bf16[8,16,4096]{2,1,0:T(8,128)(2,1)}, /*index=5*/s32[]{:T(128)}, s32[]{:T(128)}) while((s32[]{:T(128)}, f32[16,4096]{1,0:T(8,128)S(1)}, s32[]{:T(128)}, bf16[8,16,4096]{2,1,0:T(8,128)(2,1)}, ...), condition=%wide.region_13.14_spmd.clone, body=%wide.region_12.13_spmd.clone.sunk | while | flops 393220 | bytes 786533 | solution.py:31
  257.7 61.8 %while.74 = (s32[]{:T(128)}, f32[16,8,4096]{2,1,0:T(8,128)}, f32[16,8,4096]{2,1,0:T(8,128)}, f32[16,4096]{1,0:T(8,128)S(1)}, f32[16,4096]{1,0:T(8,128)}, /*index=5*/f32[16,8,16]{2,1,0:T(8,128)}, s32[]{:T(128)}) while((s32[]{:T(128)}, f32[16,8,4096]{2,1,0:T(8,128)}, f32[16,8,4096]{2,1,0:T(8,128)}, f32[16,4096]{1,0:T(8,128)S(1)}, ...), condition=%wide.region_16.17_spmd, body=%wide.region_14.16_spmd.sunk | while | flops 2064386 | bytes 1312853 | solution.py:136
  319.5 2.8 fusion.43
  323.7 10.1 %all_gather.44 = bf16[64,4096]{1,0:T(8,128)(2,1)S(1)} all-gather(bf16[8,4096]{1,0:T(8,128)(2,1)S(1)} %convolution_convert_fusion.1), channel_id=1, replica_groups=mesh['section'=4,'seq'=8] {'seq'}, dimensions={0}, use_global_device_ids=true | all-gather | bytes 589824 | tf_op jit(solution)/shard_map/all_gather | solution.py:165
  333.9 6.8 fusion.14
  340.7 13.5 %fusion.21 = bf16[64,4096]{1,0:T(8,128)(2,1)} fusion(bf16[1,1536,4096]{2,1,0:T(8,128)(2,1)} %param.40, bf16[64,4096]{1,0:T(8,128)(2,1)S(1)} %all_gather.44, bf16[1,4096,1536]{2,1,0:T(8,128)(2,1)} %param.39, f32[64,1536]{1,0:T(8,128)S(1)} %fusion.14), kind=kOutput, calls=%fused_computation.141 | convolution fusion | flops 1611464704 | bytes 26607616 | tf_op jit(solution)/shard_map/dot_general | solution.py:169
  354.8 32.6 %reduce-scatter.3.cloned.1.call-done = bf16[8,4096]{1,0:T(8,128)(2,1)} async-done(((bf16[64,4096]{1,0:T(8,128)(2,1)}), bf16[8,4096]{1,0:T(8,128)(2,1)}) %reduce-scatter.3.cloned.1.call-update) | async-done | bytes 65552 | tf_op jit(solution)/shard_map/reduce_scatter | solution.py:170
  390.1 24.1 %collective-permute-done.1 = bf16[128,4096]{1,0:T(8,128)(2,1)S(1)} collective-permute-done((bf16[128,4096]{1,0:T(8,128)(2,1)S(1)}, bf16[128,4096]{1,0:T(8,128)(2,1)S(1)}, u32[]{:S(2)}, u32[]{:S(2)}) %collective-permute-start.1) | collective-permute-done | bytes 1048608 | tf_op jit(solution)/shard_map/ppermute | solution.py:36
  415.8 5.1 collective-permute-start.2
  421.9 3.4 divide_multiply_fusion
  425.3 2.4 fusion.27
  428.0 4.4 compare_select_fusion
  433.9 66.2 %while.78 = (s32[]{:T(128)}, f32[16,4096]{1,0:T(8,128)S(1)}, f32[16,8,4096]{2,1,0:T(8,128)}, f32[16,8,4096]{2,1,0:T(8,128)}, f32[16,4096]{1,0:T(8,128)S(1)}, /*i...) while((s32[]{:T(128)}, f32[16,4096]{1,0:T(8,128)S(1)}, ...), condition=%wide.region_32.33_spmd.clone, body=%wide.region_23.32_spmd.clone.sunk | while | flops 4587530 | bytes 5150816 | solution.py:126
  433.9 1.8 constant_dynamic-slice_fusion.43
  438.0 1.8 constant_dynamic-slice_fusion.43
  442.0 1.8 constant_dynamic-slice_fusion.43
  446.0 2.1 constant_dynamic-slice_fusion.43
  450.3 2.3 constant_dynamic-slice_fusion.43
  454.9 1.8 constant_dynamic-slice_fusion.43
  458.9 1.8 constant_dynamic-slice_fusion.43
  466.9 2.0 constant_dynamic-slice_fusion.43
  471.2 1.8 constant_dynamic-slice_fusion.43
  475.2 2.0 constant_dynamic-slice_fusion.43
  479.5 1.8 constant_dynamic-slice_fusion.43
  483.5 2.0 constant_dynamic-slice_fusion.43
  487.8 1.7 constant_dynamic-slice_fusion.43
  491.8 2.1 constant_dynamic-slice_fusion.43
  496.1 1.8 constant_dynamic-slice_fusion.43
  501.1 4.7 reduce_window_sum.27
  508.5 16.1 %all-gather.23.cloned.1.call-done = bf16[128,4096]{1,0:T(8,128)(2,1)} async-done(((bf16[16,4096]{1,0:T(8,128)(2,1)}), bf16[128,4096]{1,0:T(8,128)(2,1)}) %all-gather.23.cloned.1.call-update) | async-done | bytes 1048592 | tf_op jit(solution)/shard_map/all_gather | solution.py:18
  524.6 25.3 %all-gather.21.cloned.1.call-done = bf16[128,4096]{1,0:T(8,128)(2,1)} async-done(((bf16[16,4096]{1,0:T(8,128)(2,1)}), bf16[128,4096]{1,0:T(8,128)(2,1)}) %all-gather.21.cloned.1.call-update) | async-done | bytes 1048592 | tf_op jit(solution)/shard_map/all_gather | solution.py:18
  549.9 9.6 %while.79 = (s32[]{:T(128)}, f32[16,4096]{1,0:T(8,128)S(1)}, s32[]{:T(128)}, bf16[8,16,4096]{2,1,0:T(8,128)(2,1)}, bf16[8,16,4096]{2,1,0:T(8,128)(2,1)}, /*index=5*/s32[]{:T(128)}, s32[]{:T(128)}) while((s32[]{:T(128)}, f32[16,4096]{1,0:T(8,128)S(1)}, s32[]{:T(128)}, bf16[8,16,4096]{2,1,0:T(8,128)(2,1)}, ...), condition=%wide.region_35.36_spmd.clone, body=%wide.region_34.35_spmd.clone.sunk | while | flops 393220 | bytes 786533 | solution.py:31
  561.0 61.7 %while.75 = (s32[]{:T(128)}, f32[16,8,4096]{2,1,0:T(8,128)}, f32[16,8,4096]{2,1,0:T(8,128)}, f32[16,4096]{1,0:T(8,128)S(1)}, f32[16,4096]{1,0:T(8,128)}, /*index=5*/f32[16,8,16]{2,1,0:T(8,128)}, s32[]{:T(128)}) while((s32[]{:T(128)}, f32[16,8,4096]{2,1,0:T(8,128)}, f32[16,8,4096]{2,1,0:T(8,128)}, f32[16,4096]{1,0:T(8,128)S(1)}, ...), condition=%wide.region_38.39_spmd, body=%wide.region_36.38_spmd.sunk | while | flops 2064386 | bytes 1312853 | solution.py:136
  622.8 2.8 fusion.50
  627.0 9.9 %all_gather.49 = bf16[64,4096]{1,0:T(8,128)(2,1)S(1)} all-gather(bf16[8,4096]{1,0:T(8,128)(2,1)S(1)} %convolution_convert_fusion), channel_id=1, replica_groups=mesh['section'=4,'seq'=8] {'seq'}, dimensions={0}, use_global_device_ids=true | all-gather | bytes 589824 | tf_op jit(solution)/shard_map/all_gather | solution.py:165
  637.0 6.8 fusion.12
  643.8 13.5 %fusion.24 = bf16[64,4096]{1,0:T(8,128)(2,1)} fusion(bf16[1,1536,4096]{2,1,0:T(8,128)(2,1)} %param.40, bf16[64,4096]{1,0:T(8,128)(2,1)S(1)} %all_gather.49, bf16[1,4096,1536]{2,1,0:T(8,128)(2,1)} %param.39, f32[64,1536]{1,0:T(8,128)S(1)} %fusion.12), kind=kOutput, calls=%fused_computation.142 | convolution fusion | flops 1611464704 | bytes 26607616 | tf_op jit(solution)/shard_map/dot_general | solution.py:169
  657.8 32.7 %reduce-scatter.5.cloned.1.call-done = bf16[8,4096]{1,0:T(8,128)(2,1)} async-done(((bf16[64,4096]{1,0:T(8,128)(2,1)}), bf16[8,4096]{1,0:T(8,128)(2,1)}) %reduce-scatter.5.cloned.1.call-update) | async-done | bytes 65552 | tf_op jit(solution)/shard_map/reduce_scatter | solution.py:170
  690.5 2.3 fusion.20
  (1015 shorter events, 296.5 us)
Async XLA Ops:
  6.5 347.8 %copy-start = (bf16[1,4096,16]{1,2,0:T(8,128)(2,1)S(1)}, bf16[1,4096,16]{1,2,0:T(8,128)(2,1)}, u32[]{:S(2)}) copy-start(bf16[1,4096,16]{1,2,0:T(8,128)(2,1)} %param.37) | copy-start | bytes 393220
  6.5 3.1 copy-start.1
  6.5 8.7 %copy-start.13 = (f32[1,4096,16]{1,2,0:T(8,128)S(1)}, f32[1,4096,16]{1,2,0:T(8,128)}, u32[]{:S(2)}) copy-start(f32[1,4096,16]{1,2,0:T(8,128)} %param.34) | copy-start | bytes 786436
  6.5 8.7 %copy-start.30 = (f32[1,4,4096]{2,1,0:T(4,128)S(1)}, f32[1,4,4096]{2,1,0:T(4,128)}, u32[]{:S(2)}) copy-start(f32[1,4,4096]{2,1,0:T(4,128)} %param.29) | copy-start | bytes 196612
  6.5 34.5 %all-gather.13.cloned.1.call-start = ((), (), s32[]{:S(2)}) async-start(), calls=%async_computation.4 | async-start | bytes 2654208 | tf_op jit(solution)/shard_map/all_gather | solution.py:84
  7.3 8.9 %copy-start.27 = (f32[1,4096]{1,0:T(1,128)S(1)}, f32[1,4096]{1,0:T(1,128)}, u32[]{:S(2)}) copy-start(f32[1,4096]{1,0:T(1,128)} %param.30) | copy-start | bytes 49156
  7.3 63.7 %all-gather.15.cloned.1.call-start = ((), (), s32[]{:S(2)}) async-start(), calls=%async_computation.5 | async-start | bytes 2359296 | tf_op jit(solution)/shard_map/all_gather | solution.py:85
  8.0 213.3 %all-gather.19.cloned.1.call-start = ((), (), s32[]{:S(2)}) async-start(), calls=%async_computation.7 | async-start | bytes 1179648 | tf_op jit(solution)/shard_map/all_gather | solution.py:18
  10.7 4.6 copy-start.7
  10.7 5.5 collective-permute-start
  15.3 4.3 copy-start.16
  15.4 4.3 copy-start.18
  15.4 4.3 copy-start.20
  15.4 4.3 copy-start.22
  19.7 51.3 %copy-start.47 = (f32[1,4096]{1,0:T(1,128)S(1)}, f32[1,4096]{1,0:T(1,128)}, u32[]{:S(2)}) copy-start(f32[1,4096]{1,0:T(1,128)} %param.33) | copy-start | bytes 49156
  80.9 2.4 copy-start.31
  80.9 2.4 copy-start.32
  80.9 2.4 copy-start.33
  88.3 2.4 copy-start.31
  88.3 2.4 copy-start.32
  88.3 2.4 copy-start.33
  95.7 2.4 copy-start.31
  163.5 2.4 copy-start.31
  163.5 2.4 copy-start.32
  163.5 2.4 copy-start.33
  171.1 2.4 copy-start.31
  171.1 2.4 copy-start.32
  171.2 2.4 copy-start.33
  197.9 6.5 copy-start.43
  197.9 48.6 %all-gather.17.cloned.1.call-start = ((), (), s32[]{:S(2)}) async-start(), calls=%async_computation.6 | async-start | bytes 1179648 | tf_op jit(solution)/shard_map/all_gather | solution.py:18
  204.3 183.1 %reduce-scatter.3.cloned.1.call-start = ((), (), s32[]{:S(2)}) async-start(), calls=%async_computation.2 | async-start | bytes 589824 | tf_op jit(solution)/shard_map/reduce_scatter | solution.py:170
  205.4 41.1 %copy-start.40 = (pred[128,1]{0,1:T(4,128)(4,1)}, pred[128,1]{0,1:T(4,128)(4,1)S(1)}, u32[]{:S(2)}) copy-start(pred[128,1]{0,1:T(4,128)(4,1)S(1)} %get-tuple-element.576) | copy-start | bytes 388
  257.7 61.8 %copy-start.2 = (bf16[1,128,4096]{2,1,0:T(8,128)(2,1)S(1)}, bf16[1,128,4096]{2,1,0:T(8,128)(2,1)}, u32[]{:S(2)}) copy-start(bf16[1,128,4096]{2,1,0:T(8,128)(2,1)} %param.27) | copy-start | bytes 3145732
  257.7 61.8 %copy-start.29 = (f32[1,4096]{1,0:T(1,128)S(1)}, f32[1,4096]{1,0:T(1,128)}, u32[]{:S(2)}) copy-start(f32[1,4096]{1,0:T(1,128)} %param.35) | copy-start | bytes 49156
  319.5 3.8 copy-start.41
  319.5 3.8 copy-start.45
  319.5 3.8 copy-start.49
  340.7 13.6 %copy-start.37 = (s32[128,2]{0,1:T(2,128)S(1)}, s32[128,2]{0,1:T(2,128)}, u32[]{:S(2)}) copy-start(s32[128,2]{0,1:T(2,128)} %copy-done.36) | copy-start | bytes 3076
  340.7 13.6 %copy-start.10 = (bf16[128,4096]{1,0:T(8,128)(2,1)S(1)}, bf16[128,4096]{1,0:T(8,128)(2,1)}, u32[]{:S(2)}) copy-start(bf16[128,4096]{1,0:T(8,128)(2,1)} %copy-done.9) | copy-start | bytes 3145732
  340.7 13.6 %copy-start.50 = (f32[1,4096]{1,0:T(1,128)S(1)}, f32[1,4096]{1,0:T(1,128)}, u32[]{:S(2)}) copy-start(f32[1,4096]{1,0:T(1,128)} %param.36) | copy-start | bytes 49156
  354.2 33.2 %copy-start.42 = (pred[128,1]{0,1:T(4,128)(4,1)S(1)}, pred[128,1]{0,1:T(4,128)(4,1)}, u32[]{:S(2)}) copy-start(pred[128,1]{0,1:T(4,128)(4,1)} %copy-done.40) | copy-start | bytes 388
  354.2 33.2 %copy-start.46 = (s32[128]{0:T(128)S(1)}, s32[128]{0:T(128)}, u32[]{:S(2)}) copy-start(s32[128]{0:T(128)} %convert_subtract_fusion.1) | copy-start | bytes 1540
  354.2 170.4 %all-gather.23.cloned.1.call-start = ((), (), s32[]{:S(2)}) async-start(), calls=%async_computation.9 | async-start | bytes 1179648 | tf_op jit(solution)/shard_map/all_gather | solution.py:18
  354.8 59.7 %copy-start.26 = (f32[1,4096]{1,0:T(1,128)S(1)}, f32[1,4096]{1,0:T(1,128)}, u32[]{:S(2)}) copy-start(f32[1,4096]{1,0:T(1,128)} %param.28) | copy-start | bytes 49156
  388.7 33.1 %copy-start.17 = (f32[1,1,4096]{2,1,0:T(1,128)S(1)}, f32[1,1,4096]{2,1,0:T(1,128)}, u32[]{:S(2)}) copy-start(f32[1,1,4096]{2,1,0:T(1,128)} %copy-done.16) | copy-start | bytes 49156
  388.8 33.1 %copy-start.19 = (f32[1,1,4096]{2,1,0:T(1,128)S(1)}, f32[1,1,4096]{2,1,0:T(1,128)}, u32[]{:S(2)}) copy-start(f32[1,1,4096]{2,1,0:T(1,128)} %copy-done.18) | copy-start | bytes 49156
  388.8 33.1 %copy-start.21 = (f32[1,1,4096]{2,1,0:T(1,128)S(1)}, f32[1,1,4096]{2,1,0:T(1,128)}, u32[]{:S(2)}) copy-start(f32[1,1,4096]{2,1,0:T(1,128)} %copy-done.20) | copy-start | bytes 49156
  388.8 33.1 %copy-start.23 = (f32[1,1,4096]{2,1,0:T(1,128)S(1)}, f32[1,1,4096]{2,1,0:T(1,128)}, u32[]{:S(2)}) copy-start(f32[1,1,4096]{2,1,0:T(1,128)} %copy-done.22) | copy-start | bytes 49156
  388.8 33.1 %copy-start.28 = (f32[1,4096]{1,0:T(1,128)S(1)}, f32[1,4096]{1,0:T(1,128)}, u32[]{:S(2)}) copy-start(f32[1,4096]{1,0:T(1,128)} %param.30) | copy-start | bytes 49156
  388.8 25.3 %collective-permute-start.1 = (bf16[128,4096]{1,0:T(8,128)(2,1)S(1)}, bf16[128,4096]{1,0:T(8,128)(2,1)S(1)}, u32[]{:S(2)}, u32[]{:S(2)}) collective-permute-start(bf16[128,4096]{1,0:T(8,128)(2,1)S(1)} %fusion.18), channel_id=1, source_target_pairs={{0,8},{8,16},{16,24},{24,0},{1,9},{9,17},{17,25},{25,1},{2,10},{10... | collective-permute-start | bytes 3145736 | tf_op jit(solution)/shard_map/ppermute | solution.py:36
  415.8 6.1 collective-permute-start.2
  425.3 2.7 copy-start.48
  500.1 5.7 copy-start.15
  500.8 5.9 copy-start.14
  500.8 6.7 copy-start.34
  500.9 49.0 %all-gather.21.cloned.1.call-start = ((), (), s32[]{:S(2)}) async-start(), calls=%async_computation.8 | async-start | bytes 1179648 | tf_op jit(solution)/shard_map/all_gather | solution.py:18
  507.5 183.0 %reduce-scatter.5.cloned.1.call-start = ((), (), s32[]{:S(2)}) async-start(), calls=%async_computation.3 | async-start | bytes 589824 | tf_op jit(solution)/shard_map/reduce_scatter | solution.py:170
  507.6 42.3 %copy-start.38 = (pred[128,1]{0,1:T(4,128)(4,1)}, pred[128,1]{0,1:T(4,128)(4,1)S(1)}, u32[]{:S(2)}) copy-start(pred[128,1]{0,1:T(4,128)(4,1)S(1)} %get-tuple-element.572) | copy-start | bytes 388
  561.0 61.7 %copy-start.4 = (bf16[128,4096]{1,0:T(8,128)(2,1)S(1)}, bf16[128,4096]{1,0:T(8,128)(2,1)}, u32[]{:S(2)}) copy-start(bf16[128,4096]{1,0:T(8,128)(2,1)} %copy-done.3) | copy-start | bytes 3145732
  622.8 3.8 copy-start.39
  622.8 3.8 copy-start.44
  622.8 3.8 copy-start.51
  643.8 13.5 %copy-start.35 = (s32[128,2]{0,1:T(2,128)S(1)}, s32[128,2]{0,1:T(2,128)}, u32[]{:S(2)}) copy-start(s32[128,2]{0,1:T(2,128)} %get-tuple-element.671) | copy-start | bytes 3076
  643.8 13.5 %copy-start.12 = (bf16[128,4096]{1,0:T(8,128)(2,1)S(1)}, bf16[128,4096]{1,0:T(8,128)(2,1)}, u32[]{:S(2)}) copy-start(bf16[128,4096]{1,0:T(8,128)(2,1)} %copy-done.11) | copy-start | bytes 3145732
  (74 other events, 165.7 us)
Sparse Core Ops, SparseCore 0:
  9.2 31.7 all-gather.12
  42.9 28.0 all-gather.14
  198.0 23.3 all-gather.18
  223.1 23.3 all-gather.16
  354.3 33.0 reduce-scatter.2
  501.0 23.5 all-gather.22
  526.5 23.3 all-gather.20
  657.4 33.0 reduce-scatter.4
where the time goes:
time: 706 us; the launch traced here: 700 us
  waiting for transfers between devices  222 us (31%)
  local copies, waits for them, and re-layouts  207 us (29%)
  other arithmetic  160 us (23%)
  matrix products  59.7 us (8%)
  blocking collectives  20 us (3%)
  between operations  14.2 us (2%)
  starting transfers between devices  11.4 us (2%)
    all_gather x4, waiting for transfers between devices, entering_2(): lax.all_gather(part.astype(kind), axis)  81.5 us
    reduce_scatter x2, waiting for transfers between devices, body(): lax.psum_scatter(terms.astype(jnp.bfloat16), 'seq', scatter_dimension=0,...  65.3 us
    slice x32, local copies, waits for them, and re-layouts, first_pass(): block[1][offset]  60.3 us
    reduce_sum x96, other arithmetic, first_pass(): outputs.append(jnp.sum(state * block[3][offset][:, None], axis=0))  59.7 us
    reduce_sum x32, other arithmetic, correction(): return jnp.sum(decayed * entering[None, :, :] * c_block[:, :, None], axis=1)  50.7 us
    dynamic_update_slice x64, local copies, waits for them, and re-layouts, body(): ending, local_out = lax.scan(first_pass, zeros_state, blocked)  42.5 us
    mul x32, local copies, waits for them, and re-layouts, correction(): decayed = jnp.exp(steps_block[:, None, :] * decay_rates[None, :, :])  29.4 us
    dot_general x2, matrix products, body(): terms = jnp.dot(hidden, own_down, preferred_element_type=jnp.float32)  27 us
  transfers between devices with their start and end apart: 11, of which 11 were waited for; matrix products, arithmetic and copies ran while one was open for 4% of the time, Pallas kernels for 0%

commit v1 on v0

v1 whole, which is shorter than its diff:
```python
import functools

import jax
import jax.numpy as jnp
from jax import lax
from jax.experimental import pallas as pl
from jax.experimental.pallas import tpu as pltpu
from jax.sharding import PartitionSpec as P

STEPS = 2
LANES = 128
ROWS = 8
MESH = pl.DeviceIdType.MESH
VMEM_LIMIT = 48 * 1024 * 1024


def greet(axis):
    n, me = lax.axis_size(axis), lax.axis_index(axis)
    barrier = pltpu.get_barrier_semaphore()
    for k in range(1, n):
        pl.semaphore_signal(
            barrier, inc=1, device_id={axis: lax.rem(me + k, n)}, device_id_type=MESH
        )
    pl.semaphore_wait(barrier, n - 1)


def exchange_kernel(axis, src_at, dst_at, x_ref, o_ref, send_sem, recv_sem, local_sem):
    n, me = lax.axis_size(axis), lax.axis_index(axis)
    greet(axis)
    copies = []
    for k in range(1, n):
        peer = lax.rem(me + k, n)
        copy = pltpu.make_async_remote_copy(
            src_ref=src_at(x_ref, peer),
            dst_ref=dst_at(o_ref, me),
            send_sem=send_sem.at[k],
            recv_sem=recv_sem.at[k],
            device_id={axis: peer},
            device_id_type=MESH,
        )
        copy.start()
        copies.append(copy)
    own = pltpu.make_async_copy(src_at(x_ref, me), dst_at(o_ref, me), local_sem)
    own.start()
    own.wait()
    for copy in copies:
        copy.wait()


def exchange(x, shape, src_at, dst_at, axis, cid):
    n = lax.axis_size(axis)
    return pl.pallas_call(
        functools.partial(exchange_kernel, axis, src_at, dst_at),
        out_shape=jax.ShapeDtypeStruct(shape, x.dtype),
        in_specs=[pl.BlockSpec(memory_space=pl.ANY)],
        out_specs=pl.BlockSpec(memory_space=pl.ANY),
        scratch_shapes=[
            pltpu.SemaphoreType.DMA((n,)),
            pltpu.SemaphoreType.DMA((n,)),
            pltpu.SemaphoreType.DMA,
        ],
        compiler_params=pltpu.CompilerParams(collective_id=cid, has_side_effects=True),
        name=f"exchange_{cid}",
    )(x)


def scatter_sum_kernel(axis, src_at, x_ref, o_ref, held, send_sem, recv_sem, local_sem):
    n, me = lax.axis_size(axis), lax.axis_index(axis)
    greet(axis)
    copies = []
    for k in range(1, n):
        peer = lax.rem(me + k, n)
        copy = pltpu.make_async_remote_copy(
            src_ref=src_at(x_ref, peer),
            dst_ref=held.at[k],
            send_sem=send_sem.at[k],
            recv_sem=recv_sem.at[k],
            device_id={axis: peer},
            device_id_type=MESH,
        )
        copy.start()
        copies.append(copy)
    own = pltpu.make_async_copy(src_at(x_ref, me), held.at[0], local_sem)
    own.start()
    own.wait()
    total = held[0].astype(jnp.float32)
    for k in range(1, n):
        copies[k - 1].wait()
        total = total + held[k].astype(jnp.float32)
    o_ref[...] = total


def scatter_sum(x, shape, src_at, axis, cid):
    n = lax.axis_size(axis)
    return pl.pallas_call(
        functools.partial(scatter_sum_kernel, axis, src_at),
        out_shape=jax.ShapeDtypeStruct(shape, jnp.float32),
        in_specs=[pl.BlockSpec(memory_space=pl.ANY)],
        out_specs=pl.BlockSpec(memory_space=pltpu.VMEM),
        scratch_shapes=[
            pltpu.VMEM((n,) + shape, x.dtype),
            pltpu.SemaphoreType.DMA((n,)),
            pltpu.SemaphoreType.DMA((n,)),
            pltpu.SemaphoreType.DMA,
        ],
        compiler_params=pltpu.CompilerParams(collective_id=cid, has_side_effects=True),
        name=f"scatter_sum_{cid}",
    )(x)


def row_block(size):
    return lambda ref, i: ref.at[pl.ds(pl.multiple_of(i * size, size), size), :]


def column_block(size):
    return lambda ref, i: ref.at[:, pl.ds(pl.multiple_of(i * size, size), size)]


def whole(ref, i):
    return ref


def slot_of(ref, i):
    return ref.at[i]


def scan_kernel(nstate, dt_ref, x_ref, bc_ref, a_ref, o_ref, h_ref):
    @pl.when(pl.program_id(0) == 0)
    def _():
        h_ref[...] = jnp.zeros_like(h_ref)

    rates = a_ref[...]
    width = rates.shape[1]

    def block(i, h):
        at = pl.ds(pl.multiple_of(i * ROWS, ROWS), ROWS)
        dt = dt_ref[at, :]
        u = dt * x_ref[at, :]
        bc = bc_ref[i]
        rows = []
        for k in range(ROWS):
            d = jnp.broadcast_to(dt[k : k + 1], (nstate, width))
            v = jnp.broadcast_to(u[k : k + 1], (nstate, width))
            h = jnp.exp(d * rates) * h + v * bc[:nstate, k : k + 1]
            rows.append(jnp.sum(h * bc[nstate:, k : k + 1], axis=0, keepdims=True))
        o_ref[at, :] = jnp.concatenate(rows, 0)
        return h

    h_ref[...] = lax.fori_loop(0, dt_ref.shape[0] // ROWS, block, h_ref[...])


def selective_scan(dt, x, bc, rates):
    length, width = dt.shape
    nstate = rates.shape[0]
    chunk = 128
    return pl.pallas_call(
        functools.partial(scan_kernel, nstate),
        out_shape=jax.ShapeDtypeStruct((length, width), jnp.float32),
        grid=(length // chunk,),
        in_specs=[
            pl.BlockSpec((chunk, width), lambda i: (i, 0)),
            pl.BlockSpec((chunk, width), lambda i: (i, 0)),
            pl.BlockSpec((chunk // ROWS, 2 * nstate, ROWS), lambda i: (i, 0, 0)),
            pl.BlockSpec((nstate, width), lambda i: (0, 0)),
        ],
        out_specs=pl.BlockSpec((chunk, width), lambda i: (i, 0)),
        scratch_shapes=[pltpu.VMEM((nstate, width), jnp.float32)],
        cost_estimate=pl.CostEstimate(
            flops=6 * length * width * nstate,
            bytes_accessed=12 * length * width,
            transcendentals=length * width * nstate,
        ),
        name="selective_scan",
    )(dt, x, bc, rates)


def passed_along(x, axis):
    length = lax.axis_size(axis)
    return lax.ppermute(x, axis, [(i, (i + 1) % length) for i in range(length)])


def dispatch_of(ids, blocks, capacity):
    length = ids.shape[0]
    size = length // blocks
    routed = (ids[:, 0] == 0) | (ids[:, 1] == 0)
    counted = routed.astype(jnp.float32).reshape(blocks, size)
    before = jnp.tril(jnp.ones((size, size), jnp.float32), -1)
    rank = jnp.dot(counted, before.T).reshape(length)
    slot = rank.astype(jnp.int32) + (jnp.arange(length, dtype=jnp.int32) // size) * capacity
    chosen = (jnp.arange(blocks * capacity, dtype=jnp.int32)[:, None] == slot[None, :]) & routed[
        None, :
    ]
    return chosen.astype(jnp.bfloat16), routed


def body(
    input_in_transit,
    mixer_norm_gain,
    convolution_weight,
    convolution_bias,
    input_projection,
    step_size_projection,
    step_size_bias,
    log_decay_rates,
    mixer_skip_weight,
    expert_norm_gain,
    router,
    gate_weight,
    up_weight,
    down_weight,
    expert_index_table,
):
    n, me = lax.axis_size("seq"), lax.axis_index("seq")
    experts = router.shape[2]
    rows = input_in_transit.shape[1]
    model = input_in_transit.shape[2]
    nstate = log_decay_rates.shape[2]
    rank = step_size_projection.shape[1]
    kernel = convolution_weight.shape[1]
    capacity = rows // 16
    length, width = rows * n, model // n
    slots = capacity * n
    f32, bf16 = jnp.float32, jnp.bfloat16

    def own(weight, axis):
        return lax.dynamic_slice_in_dim(weight, me * width, width, axis)

    gain = own(mixer_norm_gain[0], 0)
    taps = own(convolution_weight[0], 1)
    conv_bias = own(convolution_bias[0], 0)
    dt_bias = own(step_size_bias[0], 0)
    rates = -jnp.exp(own(log_decay_rates[0], 0)).T
    skip = own(mixer_skip_weight[0], 0)
    columns = rank + 2 * nstate
    extra = -columns % LANES
    projection = jnp.pad(input_projection[0], ((0, 0), (0, extra)))

    tokens = input_in_transit[0]
    as_float = tokens.astype(f32)
    square = jnp.sum(as_float * as_float, axis=-1)
    ids = expert_index_table[:, 0].astype(f32)
    small = jnp.concatenate(
        [ids.transpose(0, 2, 1).reshape(2 * STEPS, rows), square[None]], 0
    )
    small = jnp.pad(small, ((0, -small.shape[0] % ROWS), (0, 0)))
    small = exchange(small, (n,) + small.shape, whole, slot_of, "seq", 1)
    square = small[:, 2 * STEPS].reshape(length)
    all_ids = small[:, : 2 * STEPS].reshape(n, STEPS, 2, rows).transpose(1, 0, 3, 2)
    all_ids = all_ids.reshape(STEPS, length, 2)
    present = exchange(
        tokens, (length, width), column_block(width), row_block(rows), "seq", 2
    )

    for step in range(STEPS):
        if step:
            as_float = present.astype(f32)
            part = jnp.sum(as_float * as_float, axis=-1).reshape(n, rows)
            part = jnp.pad(part, ((0, -n % ROWS), (0, 0)))
            part = exchange(part, (n,) + part.shape, whole, slot_of, "seq", 3)
            square = jnp.sum(part, axis=0)[:n].reshape(length)
        scale = lax.rsqrt(square / model + 1e-06)
        normed = (present.astype(f32) * scale[:, None] * gain).astype(bf16)
        padded = jnp.concatenate([jnp.zeros((kernel - 1, width), bf16), normed], 0)
        convolved = conv_bias
        for tap in range(kernel):
            convolved = convolved + taps[tap] * padded[tap : tap + length].astype(f32)
        inner = jax.nn.silu(convolved)
        partial = jnp.dot(inner.astype(bf16), projection, preferred_element_type=f32).astype(bf16)
        projected = scatter_sum(partial, (rows, columns + extra), row_block(rows), "seq", 4)
        maps = projected[:, rank:columns]
        coarse = maps.astype(bf16)
        fine = (maps - coarse.astype(f32)).astype(bf16)
        sent = jnp.concatenate([projected[:, :rank].astype(bf16), coarse, fine], 1)
        sent = jnp.pad(sent, ((0, 0), (0, -sent.shape[1] % LANES)))
        everyone = exchange(sent, (length, sent.shape[1]), whole, row_block(rows), "seq", 5)
        maps = everyone[:, rank:columns].astype(f32) + everyone[
            :, columns : columns + 2 * nstate
        ].astype(f32)
        bc = maps.reshape(length // ROWS, ROWS, 2 * nstate).transpose(0, 2, 1)
        step_size = jax.nn.softplus(
            jnp.dot(everyone[:, :rank], step_size_projection[0], preferred_element_type=f32)
            + dt_bias
        )
        scanned = selective_scan(step_size, inner, bc, rates)
        mixed = (present.astype(f32) + (scanned + skip * inner)).astype(bf16)
        dispatch, routed = dispatch_of(all_ids[step], n, capacity)
        picked = jnp.dot(dispatch, mixed, preferred_element_type=f32).astype(bf16)
        last = step + 1 == STEPS
        if not last:
            moved = passed_along(mixed, "section")
            moved_ids = passed_along(all_ids[step], "section")
        full = exchange(picked, (slots, model), whole, column_block(width), "seq", 6)
        full_float = full.astype(f32)
        moe_in = (
            full_float
            * lax.rsqrt(jnp.mean(full_float * full_float, axis=-1, keepdims=True) + 1e-06)
            * expert_norm_gain[0]
        ).astype(bf16)
        logits = jnp.dot(moe_in, router[0], preferred_element_type=f32)
        slot_ids = jnp.dot(dispatch, all_ids[step].astype(bf16), preferred_element_type=f32)
        one_hot = (
            slot_ids[:, :, None] == jnp.arange(experts, dtype=jnp.int32).astype(f32)
        ).astype(f32)
        first = jnp.sum(logits * one_hot[:, 0], axis=1)
        second = jnp.sum(logits * one_hot[:, 1], axis=1)
        weight_one = jax.nn.sigmoid(first - second)
        route = jnp.where(
            slot_ids[:, 0] == 0,
            weight_one,
            jnp.where(slot_ids[:, 1] == 0, 1.0 - weight_one, jnp.zeros_like(weight_one)),
        )
        gate_part = jnp.dot(moe_in, gate_weight[0], preferred_element_type=f32)
        up_part = jnp.dot(moe_in, up_weight[0], preferred_element_type=f32)
        hidden = (jax.nn.silu(gate_part) * up_part).astype(bf16)
        terms = jnp.dot(hidden, down_weight[0], preferred_element_type=f32).astype(bf16)
        expert_out = scatter_sum(terms, (slots, width), column_block(width), "seq", 7).astype(bf16)
        new_rows = (picked.astype(f32) + route[:, None] * expert_out.astype(f32)).astype(bf16)
        if not last:
            new_rows = passed_along(new_rows, "section")
            dispatch, routed = dispatch_of(moved_ids, n, capacity)
            mixed = moved
        placed = lax.dot_general(
            dispatch, new_rows, (((0,), (0,)), ((), ())), preferred_element_type=f32
        ).astype(bf16)
        present = jnp.where(routed[:, None], placed, mixed)
    produced = exchange(present, (rows, model), row_block(rows), column_block(width), "seq", 8)
    return produced[None]


def solution(mesh):
    return jax.shard_map(
        body,
        mesh=mesh,
        in_specs=(
            P("section", "seq", None),
            P("section", None),
            P("section", None, None),
            P("section", None),
            P("section", "seq", None),
            P("section", None, "seq"),
            P("section", None),
            P("section", None, None),
            P("section", None),
            P("section", None),
            P("section", None, None),
            P("section", None, "seq"),
            P("section", None, "seq"),
            P("section", "seq", None),
            P(None, "section", "seq", None),
        ),
        out_specs=P("section", "seq", None),
        check_vma=False,
    )
```

time: 706 us -> 281 us (0.40)
  waiting for transfers between devices: 222 us -> 4.05 us
  local copies, waits for them, and re-layouts: 207 us -> 13.1 us
  Pallas kernels: 0 us -> 173 us
  other arithmetic: 160 us -> 25.9 us
  blocking collectives: 20 us -> 0 us
  between operations: 14.2 us -> 0.41 us
  starting transfers between devices: 11.4 us -> 4.23 us
    pallas_call x0 -> x14, Pallas kernels: none -> 173 us  [the longest x8 85.3 us: exchange(): pl.pallas_call(functools.partial(exchange_kernel, axis, src_at, dst_at),...]
    all_gather x6 -> x0, waiting for transfers between devices: 129 us -> none  [the longest x4 81.5 us: entering_2(): lax.all_gather(part.astype(kind), axis)]
    reduce_sum x132 -> x4, other arithmetic: 118 us -> 4.83 us  [the longest x2 2.49 us: body(): jnp.mean(full_float * full_float, axis=-1, keepdims=True) + 1e-06]
    mul x128 -> x0, local copies, waits for them, and re-layouts: 71.1 us -> none  [the longest x32 29.4 us: correction(): decayed = jnp.exp(steps_block[:, None, :] * decay_rates[None, :, :])]
    reduce_scatter x2 -> x0, waiting for transfers between devices: 65.3 us -> none  [body(): lax.psum_scatter(terms.astype(jnp.bfloat16), 'seq', scatter_dimension=0,...]
    slice x43 -> x5, local copies, waits for them, and re-layouts: 63.9 us -> 2.77 us  [the longest x2 1.83 us: body(): sent = jnp.concatenate([projected[:, :rank].astype(bf16), coarse, fine], 1)]
    dynamic_update_slice x64 -> x0, local copies, waits for them, and re-layouts: 42.5 us -> none  [body(): ending, local_out = lax.scan(first_pass, zeros_state, blocked)]
    ppermute x3, waiting for transfers between devices: 25.9 us -> 4.05 us  [passed_along(): return lax.ppermute(x, axis, [(i, (i + 1) % length) for i in range(length)])]
  transfers between devices with their start and end apart: 11 -> 3, of which waited for: 11 -> 1; matrix products, arithmetic and copies ran while one was open for 4% -> 9% of each run, Pallas kernels for 0% -> 7%
where the time goes in v1:
time: 281 us; the launch traced here: 280 us
  Pallas kernels  173 us (62%)
  matrix products  59.4 us (21%)
  other arithmetic  25.9 us (9%)
  local copies, waits for them, and re-layouts  13.1 us (5%)
  starting transfers between devices  4.23 us (2%)
  waiting for transfers between devices  4.05 us (1%)
    pallas_call x8, Pallas kernels, exchange(): pl.pallas_call(functools.partial(exchange_kernel, axis, src_at, dst_at),...  85.3 us
    pallas_call x4, Pallas kernels, scatter_sum(): pl.pallas_call(functools.partial(scatter_sum_kernel, axis, src_at), out_s...  46.1 us
    pallas_call x2, Pallas kernels, selective_scan(): pl.pallas_call(functools.partial(scan_kernel, nstate), out_shape=jax.Shap...  41.8 us
    dot_general x2, matrix products, body(): jnp.dot(hidden, down_weight[0], preferred_element_type=f32).astype(bf16)  27.1 us
    dot_general x2, matrix products, body(): gate_part = jnp.dot(moe_in, gate_weight[0], preferred_element_type=f32)  14.3 us
    convert_element_type x2, other arithmetic, body(): mixed = (present.astype(f32) + (scanned + skip * inner)).astype(bf16)  6.86 us
    dot_general x2, matrix products, body(): jnp.dot(everyone[:, :rank], step_size_projection[0], preferred_element_ty...  6.33 us
  transfers between devices with their start and end apart: 3, of which 1 were waited for; matrix products, arithmetic and copies ran while one was open for 9% of the time, Pallas kernels for 7%

profile of v1, /device:TPU:1, one launch (start us, length us, event | category | flops | bytes accessed | tf_op | source)
XLA Modules:
  0.0 280.3 jit_solution(16030751965622648476)
XLA Ops:
  0.0 1.6 multiply_reduce_fusion
  1.6 16.6 %exchange_2.1 = bf16[1024,512]{1,0:T(8,128)(2,1)} custom-call(bf16[128,4096]{1,0:T(8,128)(2,1)} %bitcast.166), custom_call_target="tpu_custom_call" | custom-call | tf_op jit(solution)/shard_map/exchange_2/pallas_call | solution.py:52
  18.2 0.6 select_maximum_fusion.x_ref
  18.8 4.8 %exchange_1.1 = f32[8,8,128]{2,1,0:T(8,128)} custom-call(f32[8,128]{1,0:T(8,128)} %select_maximum_fusion.x_ref), custom_call_target="tpu_custom_call" | custom-call | tf_op jit(solution)/shard_map/exchange_1/pallas_call | solution.py:52
  23.6 0.8 add_rsqrt_fusion
  24.3 0.7 constant_dynamic-slice_fusion.3
  25.1 0.7 constant_dynamic-slice_fusion.4
  25.8 1.5 fusion.31
  27.3 0.9 constant_dynamic-slice_fusion.2
  28.2 1.4 divide_multiply_fusion.1.x_ref
  29.6 1.3 copy-done.5
  31.0 1.6 convolution_convert_fusion.3.x_ref
  32.6 13.1 %scatter_sum_4.2 = f32[128,384]{1,0:T(8,128)} custom-call(bf16[1024,384]{1,0:T(8,128)(2,1)} %convolution_convert_fusion.3.x_ref), custom_call_target="tpu_custom_call" | custom-call | tf_op jit(solution)/shard_map/scatter_sum_4/pallas_call | solution.py:95
  45.7 0.9 subtract_convert_fusion.1
  46.6 0.9 slice.239
  47.6 0.7 fusion.113.x_ref
  48.3 12.2 %exchange_5.2 = bf16[1024,384]{1,0:T(8,128)(2,1)} custom-call(bf16[128,384]{1,0:T(8,128)(2,1)} %fusion.113.x_ref), custom_call_target="tpu_custom_call" | custom-call | tf_op jit(solution)/shard_map/exchange_5/pallas_call | solution.py:52
  60.5 1.2 add_bitcast_fusion.1
  61.8 1.9 copy.20
  63.7 1.4 negate_bitcast_fusion.a_ref
  65.1 2.7 compare_select_fusion.1.dt_ref
  67.7 20.9 %selective_scan.2 = f32[1024,512]{1,0:T(8,128)} custom-call(f32[1024,512]{1,0:T(8,128)} %compare_select_fusion.1.dt_ref, f32[1024,512]{1,0:T(8,128)} %copy-done.5, f32[128,32,8]{2,1,0:T(8,128)} %bitcast.168, f32[16,512]{1,0:T(8,128)} %negate_bitcast_fusion.a_ref), custom_call_target="tpu_custom_call" | custom-call | flops 50331648 | bytes 6291456 | tf_op jit(solution)/shard_map/selective_scan/pallas_call | solution.py:156
  88.7 3.3 %fusion.32 = bf16[1024,512]{1,0:T(8,128)(2,1)S(1)} fusion(bf16[1024,512]{1,0:T(8,128)(2,1)S(1)} %copy-done.4, f32[1024,512]{1,0:T(8,128)} %selective_scan.2, f32[512]{0:T(512)S(1)} %bitcast.203, bf16[1024,512]{1,0:T(8,128)(2,1)S(1)} %fusion.31, f32[512]{0:T(512)S(1)} %bitcast.197, f32[512]{0:T(512)S(1)} %bitcast.189, f32[512]{0:T(512)S(1)} %bitcast.193, ...), kind=kLoop, calls=%fused_computation.27 | loop fusion | flops 11010048 | bytes 5255168 | tf_op jit(solution)/shard_map/convert_element_type | solution.py:285
  92.0 1.4 collective-permute-start.2
  93.3 1.5 collective-permute-start
  95.1 0.9 convolution_convert_fusion.5.x_ref
  96.2 9.7 %exchange_6.2 = bf16[64,4096]{1,0:T(8,128)(2,1)} custom-call(bf16[64,512]{1,0:T(8,128)(2,1)} %convolution_convert_fusion.5.x_ref), custom_call_target="tpu_custom_call" | custom-call | tf_op jit(solution)/shard_map/exchange_6/pallas_call | solution.py:52
  105.9 1.2 fusion.44
  107.2 0.2 fusion.41
  107.6 7.2 %fusion.10 = f32[64,1536]{1,0:T(8,128)S(1)} fusion(bf16[1,4096,1536]{2,1,0:T(8,128)(2,1)} %param.26, bf16[64,4096]{1,0:T(8,128)(2,1)} %exchange_6.2, f32[4096]{0:T(1024)S(1)} %bitcast.172, f32[64]{0:T(128)S(1)} %add_rsqrt_fusion.2), kind=kOutput, calls=%fused_computation.10 | convolution fusion | flops 806354944 | bytes 13517056 | tf_op jit(solution)/shard_map/dot_general | solution.py:312
  114.8 13.6 %fusion.12.x_ref = bf16[64,4096]{1,0:T(8,128)(2,1)} fusion(bf16[1,1536,4096]{2,1,0:T(8,128)(2,1)} %param.28, bf16[1,4096,1536]{2,1,0:T(8,128)(2,1)} %param.27, f32[64,1536]{1,0:T(8,128)S(1)} %fusion.10, bf16[64,4096]{1,0:T(8,128)(2,1)S(1)} %copy-done.2, f32[4096]{0:T(1024)S(1)} %bitcast.173, f32[64]{0:T(128)S(1)} %add_rsqrt_fusion.2), kind=kOutput, calls=%fused_computation.14 | convolution fusion | flops 1612513280 | bytes 26624256 | tf_op jit(solution)/shard_map/dot_general | solution.py:315
  128.4 10.0 %scatter_sum_7.2 = f32[64,512]{1,0:T(8,128)} custom-call(bf16[64,4096]{1,0:T(8,128)(2,1)} %fusion.12.x_ref), custom_call_target="tpu_custom_call" | custom-call | tf_op jit(solution)/shard_map/scatter_sum_7/pallas_call | solution.py:95
  138.4 0.3 fusion.132
  138.8 1.0 add_convert_fusion.1
  139.8 1.4 collective-permute-start.1
  141.1 0.2 fusion.42
  141.3 4.0 %collective-permute-done.1 = bf16[64,512]{1,0:T(8,128)(2,1)S(1)} collective-permute-done((bf16[64,512]{1,0:T(8,128)(2,1)S(1)}, bf16[64,512]{1,0:T(8,128)(2,1)S(1)}, u32[]{:S(2)}, u32[]{:S(2)}) %collective-permute-start.1) | collective-permute-done | bytes 65568 | tf_op jit(solution)/shard_map/ppermute | solution.py:179
  145.4 2.5 fusion.33
  147.9 5.4 %exchange_3.1 = f32[8,8,128]{2,1,0:T(8,128)} custom-call(f32[8,128]{1,0:T(8,128)} %bitcast.209), custom_call_target="tpu_custom_call" | custom-call | tf_op jit(solution)/shard_map/exchange_3/pallas_call | solution.py:52
  153.3 0.8 reduce_sum.86
  154.1 0.3 fusion.35
  154.4 1.4 divide_multiply_fusion.x_ref
  155.8 1.3 copy-done.6
  157.1 1.7 convolution_convert_fusion.2.x_ref
  158.8 13.1 %scatter_sum_4.3 = f32[128,384]{1,0:T(8,128)} custom-call(bf16[1024,384]{1,0:T(8,128)(2,1)} %convolution_convert_fusion.2.x_ref), custom_call_target="tpu_custom_call" | custom-call | tf_op jit(solution)/shard_map/scatter_sum_4/pallas_call | solution.py:95
  171.9 0.9 subtract_convert_fusion
  172.8 0.9 slice.238
  173.8 0.7 fusion.115.x_ref
  174.5 12.2 %exchange_5.3 = bf16[1024,384]{1,0:T(8,128)(2,1)} custom-call(bf16[128,384]{1,0:T(8,128)(2,1)} %fusion.115.x_ref), custom_call_target="tpu_custom_call" | custom-call | tf_op jit(solution)/shard_map/exchange_5/pallas_call | solution.py:52
  186.7 1.2 add_bitcast_fusion
  187.9 3.7 %compare_select_fusion.dt_ref = f32[1024,512]{1,0:T(8,128)} fusion(f32[512]{0:T(512)S(1)} %bitcast.212, bf16[1024,384]{1,0:T(8,128)(2,1)} %exchange_5.3, bf16[1,256,512]{2,1,0:T(8,128)(2,1)S(1)} %copy-done), kind=kOutput, calls=%fused_computation.12 | convolution fusion | flops 272105472 | bytes 2885632 | tf_op jit(solution)/shard_map/dot_general | solution.py:281
  191.6 2.0 copy.21
  193.5 20.8 %selective_scan.3 = f32[1024,512]{1,0:T(8,128)} custom-call(f32[1024,512]{1,0:T(8,128)} %compare_select_fusion.dt_ref, f32[1024,512]{1,0:T(8,128)} %copy-done.6, f32[128,32,8]{2,1,0:T(8,128)} %bitcast.169, f32[16,512]{1,0:T(8,128)} %negate_bitcast_fusion.a_ref), custom_call_target="tpu_custom_call" | custom-call | flops 50331648 | bytes 6291456 | tf_op jit(solution)/shard_map/selective_scan/pallas_call | solution.py:156
  214.4 3.6 %fusion.36 = bf16[1024,512]{1,0:T(8,128)(2,1)S(1)} fusion(bf16[1024,512]{1,0:T(8,128)(2,1)} %copy-done.7, f32[1024,512]{1,0:T(8,128)} %selective_scan.3, f32[512]{0:T(512)S(1)} %bitcast.204, bf16[1024,512]{1,0:T(8,128)(2,1)S(1)} %fusion.35, f32[512]{0:T(512)S(1)} %bitcast.199, f32[512]{0:T(512)S(1)} %bitcast.191, f32[512]{0:T(512)S(1)} %bitcast.195, ...), kind=kLoop, calls=%fused_computation.31 | loop fusion | flops 11010048 | bytes 5255168 | tf_op jit(solution)/shard_map/convert_element_type | solution.py:285
  218.0 0.9 convolution_convert_fusion.4.x_ref
  218.8 9.4 %exchange_6.3 = bf16[64,4096]{1,0:T(8,128)(2,1)} custom-call(bf16[64,512]{1,0:T(8,128)(2,1)} %convolution_convert_fusion.4.x_ref), custom_call_target="tpu_custom_call" | custom-call | tf_op jit(solution)/shard_map/exchange_6/pallas_call | solution.py:52
  228.3 1.2 fusion.47
  229.5 7.2 %fusion.8 = f32[64,1536]{1,0:T(8,128)S(1)} fusion(bf16[1,4096,1536]{2,1,0:T(8,128)(2,1)} %param.26, bf16[64,4096]{1,0:T(8,128)(2,1)} %exchange_6.3, f32[64]{0:T(128)S(1)} %add_rsqrt_fusion.1, f32[4096]{0:T(1024)S(1)} %bitcast.175), kind=kOutput, calls=%fused_computation.8 | convolution fusion | flops 806354944 | bytes 13517056 | tf_op jit(solution)/shard_map/dot_general | solution.py:312
  236.7 0.3 fusion.128
  237.1 13.6 %fusion.15.x_ref = bf16[64,4096]{1,0:T(8,128)(2,1)} fusion(bf16[1,1536,4096]{2,1,0:T(8,128)(2,1)} %param.28, bf16[1,4096,1536]{2,1,0:T(8,128)(2,1)} %param.27, f32[64,1536]{1,0:T(8,128)S(1)} %fusion.8, bf16[64,4096]{1,0:T(8,128)(2,1)S(1)} %copy-done.3, f32[64]{0:T(128)S(1)} %add_rsqrt_fusion.1, f32[4096]{0:T(1024)S(1)} %bitcast.177), kind=kOutput, calls=%fused_computation.15 | convolution fusion | flops 1612513280 | bytes 26624256 | tf_op jit(solution)/shard_map/dot_general | solution.py:315
  250.6 10.0 %scatter_sum_7.3 = f32[64,512]{1,0:T(8,128)} custom-call(bf16[64,4096]{1,0:T(8,128)(2,1)} %fusion.15.x_ref), custom_call_target="tpu_custom_call" | custom-call | tf_op jit(solution)/shard_map/scatter_sum_7/pallas_call | solution.py:95
  260.6 2.4 fusion.37.x_ref
  263.1 15.0 %exchange_8.1 = bf16[128,4096]{1,0:T(8,128)(2,1)} custom-call(bf16[1024,512]{1,0:T(8,128)(2,1)} %fusion.37.x_ref), custom_call_target="tpu_custom_call" | custom-call | tf_op jit(solution)/shard_map/exchange_8/pallas_call | solution.py:52
  278.0 2.3 copy.37
  (55 shorter events, 0.9 us)
Async XLA Ops:
  0.0 65.1 %copy-start = (bf16[1,256,512]{2,1,0:T(8,128)(2,1)S(1)}, bf16[1,256,512]{2,1,0:T(8,128)(2,1)}, u32[]{:S(2)}) copy-start(bf16[1,256,512]{2,1,0:T(8,128)(2,1)} %param.20) | copy-start | bytes 786436
  0.0 18.1 %copy-start.14 = (s32[2,1,128,2]{2,3,1,0:T(2,128)S(1)}, s32[2,1,128,2]{2,3,1,0:T(2,128)}, u32[]{:S(2)}) copy-start(s32[2,1,128,2]{2,3,1,0:T(2,128)} %param.29) | copy-start | bytes 6148
  27.3 3.7 %copy-start.9 = (bf16[1,512,288]{1,2,0:T(8,128)(2,1)S(1)}, bf16[1,512,288]{1,2,0:T(8,128)(2,1)}, u32[]{:S(2)}) copy-start(bf16[1,512,288]{1,2,0:T(8,128)(2,1)} %param.19) | copy-start | bytes 884740
  29.6 1.4 copy-start.5
  60.5 4.6 %copy-start.8 = (bf16[1024,384]{1,0:T(8,128)(2,1)S(1)}, bf16[1024,384]{1,0:T(8,128)(2,1)}, u32[]{:S(2)}) copy-start(bf16[1024,384]{1,0:T(8,128)(2,1)} %exchange_5.2) | copy-start | bytes 2359300
  67.7 20.9 %copy-start.4 = (bf16[1024,512]{1,0:T(8,128)(2,1)S(1)}, bf16[1024,512]{1,0:T(8,128)(2,1)}, u32[]{:S(2)}) copy-start(bf16[1024,512]{1,0:T(8,128)(2,1)} %exchange_2.1) | copy-start | bytes 3145732
  88.7 4.6 %slice-start = ((f32[8,8,128]{2,1,0:T(8,128)}), f32[8,4,128]{2,1,0:T(4,128)S(1)}, s32[]{:S(2)}) async-start(f32[8,8,128]{2,1,0:T(8,128)} %exchange_1.1), calls=%async_computation | async-start | bytes 32768 | tf_op jit(solution)/shard_map/slice | solution.py:248
  92.0 15.6 %copy-start.11 = (f32[1,4096]{1,0:T(1,128)S(1)}, f32[1,4096]{1,0:T(1,128)}, u32[]{:S(2)}) copy-start(f32[1,4096]{1,0:T(1,128)} %param.24) | copy-start | bytes 49156
  92.0 53.4 %collective-permute-start.2 = (bf16[1024,512]{1,0:T(8,128)(2,1)S(1)}, bf16[1024,512]{1,0:T(8,128)(2,1)}, u32[]{:S(2)}, u32[]{:S(2)}) collective-permute-start(bf16[1024,512]{1,0:T(8,128)(2,1)S(1)} %fusion.32), channel_id=1, source_target_pairs={{0,8},{8,16},{16,24},{24,0},{1,9},{9,17},{17,25},{25,1},{2,10},{10... | collective-permute-start | bytes 3145736 | tf_op jit(solution)/shard_map/ppermute | solution.py:179
  93.3 47.8 %collective-permute-start = (f32[1024,2]{0,1:T(2,128)S(1)}, f32[1024,2]{0,1:T(2,128)S(1)}, u32[]{:S(2)}, u32[]{:S(2)}) collective-permute-start(f32[1024,2]{0,1:T(2,128)S(1)} %bitcast.200), channel_id=1, source_target_pairs={{0,8},{8,16},{16,24},{24,0},{1,9},{9,17},{17,25},{25,1},{2,10},{10... | collective-permute-start | bytes 24584 | tf_op jit(solution)/shard_map/ppermute | solution.py:179
  107.6 7.2 %copy-start.2 = (bf16[64,4096]{1,0:T(8,128)(2,1)S(1)}, bf16[64,4096]{1,0:T(8,128)(2,1)}, u32[]{:S(2)}) copy-start(bf16[64,4096]{1,0:T(8,128)(2,1)} %exchange_6.2) | copy-start | bytes 1572868
  114.8 23.6 %copy-start.15 = (bf16[1,4096,16]{1,2,0:T(8,128)(2,1)S(1)}, bf16[1,4096,16]{1,2,0:T(8,128)(2,1)}, u32[]{:S(2)}) copy-start(bf16[1,4096,16]{1,2,0:T(8,128)(2,1)} %param.25) | copy-start | bytes 393220
  114.8 24.0 %copy-start.13 = (bf16[64,512]{1,0:T(8,128)(2,1)S(1)}, bf16[64,512]{1,0:T(8,128)(2,1)}, u32[]{:S(2)}) copy-start(bf16[64,512]{1,0:T(8,128)(2,1)} %convolution_convert_fusion.5.x_ref) | copy-start | bytes 196612
  139.8 5.6 %collective-permute-start.1 = (bf16[64,512]{1,0:T(8,128)(2,1)S(1)}, bf16[64,512]{1,0:T(8,128)(2,1)S(1)}, u32[]{:S(2)}, u32[]{:S(2)}) collective-permute-start(bf16[64,512]{1,0:T(8,128)(2,1)S(1)} %add_convert_fusion.1), channel_id=1, source_target_pairs={{0,8},{8,16},{16,24},{24,0},{1,9},{9,17},{17,25},{25,1},{2,10},{10... | collective-permute-start | bytes 196616 | tf_op jit(solution)/shard_map/ppermute | solution.py:179
  147.9 7.9 %copy-start.7 = (bf16[1024,512]{1,0:T(8,128)(2,1)}, bf16[1024,512]{1,0:T(8,128)(2,1)S(1)}, u32[]{:S(2)}) copy-start(bf16[1024,512]{1,0:T(8,128)(2,1)S(1)} %get-tuple-element.22) | copy-start | bytes 3145732
  154.4 2.7 copy-start.10
  155.8 1.4 copy-start.6
  229.5 7.2 %copy-start.3 = (bf16[64,4096]{1,0:T(8,128)(2,1)S(1)}, bf16[64,4096]{1,0:T(8,128)(2,1)}, u32[]{:S(2)}) copy-start(bf16[64,4096]{1,0:T(8,128)(2,1)} %exchange_6.3) | copy-start | bytes 1572868
  229.5 7.2 %copy-start.16 = (bf16[1,4096,16]{1,2,0:T(8,128)(2,1)S(1)}, bf16[1,4096,16]{1,2,0:T(8,128)(2,1)}, u32[]{:S(2)}) copy-start(bf16[1,4096,16]{1,2,0:T(8,128)(2,1)} %param.25) | copy-start | bytes 393220
  237.1 23.5 %copy-start.12 = (bf16[64,512]{1,0:T(8,128)(2,1)S(1)}, bf16[64,512]{1,0:T(8,128)(2,1)}, u32[]{:S(2)}) copy-start(bf16[64,512]{1,0:T(8,128)(2,1)} %convolution_convert_fusion.4.x_ref) | copy-start | bytes 196612
  260.6 19.7 %copy-start.1 = (bf16[1,256,512]{2,1,0:T(8,128)(2,1)S(1)}, bf16[1,256,512]{2,1,0:T(8,128)(2,1)}, u32[]{:S(2)}) copy-start(bf16[1,256,512]{2,1,0:T(8,128)(2,1)} %param.20) | copy-start | bytes 786436

commit v2 on v1

--- a/solution.py
+++ b/solution.py
@@ -10,8 +10,9 @@
 STEPS = 2
 LANES = 128
 ROWS = 8
+LOG2E = 1.4426950408889634
 MESH = pl.DeviceIdType.MESH
-VMEM_LIMIT = 48 * 1024 * 1024
+SMALL_VMEM = 8 * 1024 * 1024
 
 
 def greet(axis):
@@ -24,49 +25,115 @@
     pl.semaphore_wait(barrier, n - 1)
 
 
-def exchange_kernel(axis, src_at, dst_at, x_ref, o_ref, send_sem, recv_sem, local_sem):
+def exchange_kernel(axis, parts, *refs):
     n, me = lax.axis_size(axis), lax.axis_index(axis)
+    count = len(parts)
+    send_sem, recv_sem, local_sem = refs[2 * count :]
     greet(axis)
     copies = []
     for k in range(1, n):
         peer = lax.rem(me + k, n)
-        copy = pltpu.make_async_remote_copy(
-            src_ref=src_at(x_ref, peer),
-            dst_ref=dst_at(o_ref, me),
-            send_sem=send_sem.at[k],
-            recv_sem=recv_sem.at[k],
-            device_id={axis: peer},
-            device_id_type=MESH,
-        )
-        copy.start()
-        copies.append(copy)
-    own = pltpu.make_async_copy(src_at(x_ref, me), dst_at(o_ref, me), local_sem)
-    own.start()
-    own.wait()
+        for p, (src_at, dst_at) in enumerate(parts):
+            copy = pltpu.make_async_remote_copy(
+                src_ref=src_at(refs[p], peer),
+                dst_ref=dst_at(refs[count + p], me),
+                send_sem=send_sem.at[p, k],
+                recv_sem=recv_sem.at[p, k],
+                device_id={axis: peer},
+                device_id_type=MESH,
+            )
+            copy.start()
+            copies.append(copy)
+    for p, (src_at, dst_at) in enumerate(parts):
+        own = pltpu.make_async_copy(
+            src_at(refs[p], me), dst_at(refs[count + p], me), local_sem.at[p]
+        )
+        own.start()
+        copies.append(own)
     for copy in copies:
         copy.wait()
 
 
-def exchange(x, shape, src_at, dst_at, axis, cid):
-    n = lax.axis_size(axis)
+def exchange(xs, shapes, parts, axis, cid):
+    n, count = lax.axis_size(axis), len(xs)
     return pl.pallas_call(
-        functools.partial(exchange_kernel, axis, src_at, dst_at),
+        functools.partial(exchange_kernel, axis, parts),
+        out_shape=[jax.ShapeDtypeStruct(shape, x.dtype) for x, shape in zip(xs, shapes)],
+        in_specs=[pl.BlockSpec(memory_space=pl.ANY)] * count,
+        out_specs=[pl.BlockSpec(memory_space=pl.ANY)] * count,
+        scratch_shapes=[
+            pltpu.SemaphoreType.DMA((count, n)),
+            pltpu.SemaphoreType.DMA((count, n)),
+            pltpu.SemaphoreType.DMA((count,)),
+        ],
+        compiler_params=pltpu.CompilerParams(
+            collective_id=cid, has_side_effects=True, vmem_limit_bytes=SMALL_VMEM
+        ),
+        name=f"exchange_{cid}",
+    )(*xs)
+
+
+def spread(axis, block, place, o_ref, send_sem, recv_sem, relay_send, relay_recv, local_sem):
+    n, me = lax.axis_size(axis), lax.axis_index(axis)
+    partner = me + 1 - 2 * lax.rem(me, 2)
+
+    def send(source, at, target, sent, received):
+        copy = pltpu.make_async_remote_copy(
+            src_ref=source,
+            dst_ref=place(o_ref, at),
+            send_sem=sent,
+            recv_sem=received,
+            device_id={axis: target},
+            device_id_type=MESH,
+        )
+        copy.start()
+        return copy
+
+    far = [
+        send(block, me, lax.rem(me + 2 * k, n), send_sem.at[k], recv_sem.at[k])
+        for k in range(1, n // 2)
+    ]
+    near = [send(block, me, partner, relay_send.at[0], relay_recv.at[0])]
+    own = pltpu.make_async_copy(block, place(o_ref, me), local_sem)
+    own.start()
+    for k in range(1, n // 2):
+        far[k - 1].wait_recv()
+        source = lax.rem(me + n - 2 * k, n)
+        near.append(
+            send(place(o_ref, source), source, partner, relay_send.at[k], relay_recv.at[k])
+        )
+    for copy in far:
+        copy.wait_send()
+    for copy in near:
+        copy.wait()
+    own.wait()
+
+
+def spread_scratch(n):
+    return [pltpu.SemaphoreType.DMA((n // 2,))] * 4 + [pltpu.SemaphoreType.DMA]
+
+
+def gather_kernel(axis, place, x_ref, o_ref, *sems):
+    greet(axis)
+    spread(axis, x_ref, place, o_ref, *sems)
+
+
+def gather(x, shape, place, axis, cid):
+    return pl.pallas_call(
+        functools.partial(gather_kernel, axis, place),
         out_shape=jax.ShapeDtypeStruct(shape, x.dtype),
         in_specs=[pl.BlockSpec(memory_space=pl.ANY)],
         out_specs=pl.BlockSpec(memory_space=pl.ANY),
-        scratch_shapes=[
-            pltpu.SemaphoreType.DMA((n,)),
-            pltpu.SemaphoreType.DMA((n,)),
-            pltpu.SemaphoreType.DMA,
-        ],
-        compiler_params=pltpu.CompilerParams(collective_id=cid, has_side_effects=True),
-        name=f"exchange_{cid}",
+        scratch_shapes=spread_scratch(lax.axis_size(axis)),
+        compiler_params=pltpu.CompilerParams(
+            collective_id=cid, has_side_effects=True, vmem_limit_bytes=SMALL_VMEM
+        ),
+        name=f"gather_{cid}",
     )(x)
 
 
-def scatter_sum_kernel(axis, src_at, x_ref, o_ref, held, send_sem, recv_sem, local_sem):
+def reduce_here(axis, src_at, x_ref, held, send_sem, recv_sem, local_sem):
     n, me = lax.axis_size(axis), lax.axis_index(axis)
-    greet(axis)
     copies = []
     for k in range(1, n):
         peer = lax.rem(me + k, n)
@@ -87,27 +154,65 @@
     for k in range(1, n):
         copies[k - 1].wait()
         total = total + held[k].astype(jnp.float32)
-    o_ref[...] = total
+    return total
+
+
+def reduce_scratch(n, shape, dtype):
+    return [
+        pltpu.VMEM((n,) + shape, dtype),
+        pltpu.SemaphoreType.DMA((n,)),
+        pltpu.SemaphoreType.DMA((n,)),
+        pltpu.SemaphoreType.DMA,
+    ]
+
+
+def scatter_sum_kernel(axis, src_at, x_ref, o_ref, *scratch):
+    greet(axis)
+    o_ref[...] = reduce_here(axis, src_at, x_ref, *scratch)
 
 
 def scatter_sum(x, shape, src_at, axis, cid):
-    n = lax.axis_size(axis)
     return pl.pallas_call(
         functools.partial(scatter_sum_kernel, axis, src_at),
         out_shape=jax.ShapeDtypeStruct(shape, jnp.float32),
         in_specs=[pl.BlockSpec(memory_space=pl.ANY)],
         out_specs=pl.BlockSpec(memory_space=pltpu.VMEM),
-        scratch_shapes=[
-            pltpu.VMEM((n,) + shape, x.dtype),
-            pltpu.SemaphoreType.DMA((n,)),
-            pltpu.SemaphoreType.DMA((n,)),
-            pltpu.SemaphoreType.DMA,
-        ],
-        compiler_params=pltpu.CompilerParams(collective_id=cid, has_side_effects=True),
+        scratch_shapes=reduce_scratch(lax.axis_size(axis), shape, x.dtype),
+        compiler_params=pltpu.CompilerParams(
+            collective_id=cid, has_side_effects=True, vmem_limit_bytes=SMALL_VMEM
+        ),
         name=f"scatter_sum_{cid}",
     )(x)
 
 
+def project_kernel(axis, src_at, place, rank, x_ref, o_ref, held, s1, s2, s3, stage, *sems):
+    greet(axis)
+    total = reduce_here(axis, src_at, x_ref, held, s1, s2, s3)
+    end = total.shape[0]
+    stage[:end, :] = total.astype(jnp.bfloat16)
+    maps = total[rank:]
+    stage[end:, :] = (maps - maps.astype(jnp.bfloat16).astype(jnp.float32)).astype(jnp.bfloat16)
+    spread(axis, stage, place, o_ref, *sems)
+
+
+def project(x, rank, block, axis, cid):
+    n, (rows, length) = lax.axis_size(axis), x.shape
+    tall = 2 * rows - rank
+    return pl.pallas_call(
+        functools.partial(project_kernel, axis, column_block(block), column_block(block), rank),
+        out_shape=jax.ShapeDtypeStruct((tall, length), x.dtype),
+        in_specs=[pl.BlockSpec(memory_space=pl.ANY)],
+        out_specs=pl.BlockSpec(memory_space=pl.ANY),
+        scratch_shapes=reduce_scratch(n, (rows, block), x.dtype)
+        + [pltpu.VMEM((tall, block), x.dtype)]
+        + spread_scratch(n),
+        compiler_params=pltpu.CompilerParams(
+            collective_id=cid, has_side_effects=True, vmem_limit_bytes=SMALL_VMEM
+        ),
+        name=f"project_{cid}",
+    )(x)
+
+
 def row_block(size):
     return lambda ref, i: ref.at[pl.ds(pl.multiple_of(i * size, size), size), :]
 
@@ -122,6 +227,28 @@
 
 def slot_of(ref, i):
     return ref.at[i]
+
+
+def folded(parts):
+    sub = lax.broadcasted_iota(jnp.int32, parts[0].shape, 0)
+    reach = ROWS // 2
+    while reach:
+        low = (sub // reach) % 2 == 0
+        half = len(parts) // 2
+        merged = []
+        for a, b in zip(parts[:half], parts[half:]):
+            keep = jnp.where(low, a, b)
+            give = jnp.where(low, b, a)
+            if reach == ROWS // 2:
+                moved = pltpu.roll(give, reach, 0)
+            else:
+                moved = jnp.where(
+                    low, pltpu.roll(give, ROWS - reach, 0), pltpu.roll(give, reach, 0)
+                )
+            merged.append(keep + moved)
+        parts = merged
+        reach //= 2
+    return parts[0]
 
 
 def scan_kernel(nstate, dt_ref, x_ref, bc_ref, a_ref, o_ref, h_ref):
@@ -129,30 +256,40 @@
     def _():
         h_ref[...] = jnp.zeros_like(h_ref)
 
-    rates = a_ref[...]
-    width = rates.shape[1]
-
-    def block(i, h):
-        at = pl.ds(pl.multiple_of(i * ROWS, ROWS), ROWS)
-        dt = dt_ref[at, :]
-        u = dt * x_ref[at, :]
-        bc = bc_ref[i]
-        rows = []
+    groups = nstate // ROWS
+    chunk = dt_ref.shape[0]
+    tile = (ROWS, dt_ref.shape[1])
+    rates = [a_ref[g * ROWS : (g + 1) * ROWS, :] for g in range(groups)]
+
+    def block(i, states):
+        states = list(states)
+        base = pl.multiple_of(i * ROWS, ROWS)
+        bc = pltpu.roll(bc_ref[...], lax.rem(chunk - i * ROWS, chunk), 1)
+        parts = []
         for k in range(ROWS):
-            d = jnp.broadcast_to(dt[k : k + 1], (nstate, width))
-            v = jnp.broadcast_to(u[k : k + 1], (nstate, width))
-            h = jnp.exp(d * rates) * h + v * bc[:nstate, k : k + 1]
-            rows.append(jnp.sum(h * bc[nstate:, k : k + 1], axis=0, keepdims=True))
-        o_ref[at, :] = jnp.concatenate(rows, 0)
-        return h
-
-    h_ref[...] = lax.fori_loop(0, dt_ref.shape[0] // ROWS, block, h_ref[...])
+            d = jnp.broadcast_to(dt_ref[pl.ds(base + k, 1), :], tile)
+            v = d * jnp.broadcast_to(x_ref[pl.ds(base + k, 1), :], tile)
+            total = None
+            for g in range(groups):
+                b = bc[g * ROWS : (g + 1) * ROWS, k : k + 1]
+                c = bc[nstate + g * ROWS : nstate + (g + 1) * ROWS, k : k + 1]
+                states[g] = jnp.exp2(d * rates[g]) * states[g] + v * b
+                term = states[g] * c
+                total = term if total is None else total + term
+            parts.append(total)
+        o_ref[pl.ds(base, ROWS), :] = folded(parts)
+        return tuple(states)
+
+    states = tuple(h_ref[g * ROWS : (g + 1) * ROWS, :] for g in range(groups))
+    states = lax.fori_loop(0, chunk // ROWS, block, states)
+    for g in range(groups):
+        h_ref[g * ROWS : (g + 1) * ROWS, :] = states[g]
 
 
 def selective_scan(dt, x, bc, rates):
     length, width = dt.shape
     nstate = rates.shape[0]
-    chunk = 128
+    chunk = LANES
     return pl.pallas_call(
         functools.partial(scan_kernel, nstate),
         out_shape=jax.ShapeDtypeStruct((length, width), jnp.float32),
@@ -160,11 +297,12 @@
         in_specs=[
             pl.BlockSpec((chunk, width), lambda i: (i, 0)),
             pl.BlockSpec((chunk, width), lambda i: (i, 0)),
-            pl.BlockSpec((chunk // ROWS, 2 * nstate, ROWS), lambda i: (i, 0, 0)),
+            pl.BlockSpec((2 * nstate, chunk), lambda i: (0, i)),
             pl.BlockSpec((nstate, width), lambda i: (0, 0)),
         ],
         out_specs=pl.BlockSpec((chunk, width), lambda i: (i, 0)),
         scratch_shapes=[pltpu.VMEM((nstate, width), jnp.float32)],
+        compiler_params=pltpu.CompilerParams(vmem_limit_bytes=SMALL_VMEM),
         cost_estimate=pl.CostEstimate(
             flops=6 * length * width * nstate,
             bytes_accessed=12 * length * width,
@@ -229,11 +367,9 @@
     taps = own(convolution_weight[0], 1)
     conv_bias = own(convolution_bias[0], 0)
     dt_bias = own(step_size_bias[0], 0)
-    rates = -jnp.exp(own(log_decay_rates[0], 0)).T
+    rates = -LOG2E * jnp.exp(own(log_decay_rates[0], 0)).T
     skip = own(mixer_skip_weight[0], 0)
     columns = rank + 2 * nstate
-    extra = -columns % LANES
-    projection = jnp.pad(input_projection[0], ((0, 0), (0, extra)))
 
     tokens = input_in_transit[0]
     as_float = tokens.astype(f32)
@@ -243,20 +379,22 @@
         [ids.transpose(0, 2, 1).reshape(2 * STEPS, rows), square[None]], 0
     )
     small = jnp.pad(small, ((0, -small.shape[0] % ROWS), (0, 0)))
-    small = exchange(small, (n,) + small.shape, whole, slot_of, "seq", 1)
+    small, present = exchange(
+        [small, tokens],
+        [(n,) + small.shape, (length, width)],
+        [(whole, slot_of), (column_block(width), row_block(rows))],
+        "seq",
+        1,
+    )
     square = small[:, 2 * STEPS].reshape(length)
     all_ids = small[:, : 2 * STEPS].reshape(n, STEPS, 2, rows).transpose(1, 0, 3, 2)
     all_ids = all_ids.reshape(STEPS, length, 2)
-    present = exchange(
-        tokens, (length, width), column_block(width), row_block(rows), "seq", 2
-    )
-
     for step in range(STEPS):
         if step:
             as_float = present.astype(f32)
             part = jnp.sum(as_float * as_float, axis=-1).reshape(n, rows)
             part = jnp.pad(part, ((0, -n % ROWS), (0, 0)))
-            part = exchange(part, (n,) + part.shape, whole, slot_of, "seq", 3)
+            (part,) = exchange([part], [(n,) + part.shape], [(whole, slot_of)], "seq", 3)
             square = jnp.sum(part, axis=0)[:n].reshape(length)
         scale = lax.rsqrt(square / model + 1e-06)
         normed = (present.astype(f32) * scale[:, None] * gain).astype(bf16)
@@ -265,20 +403,21 @@
         for tap in range(kernel):
             convolved = convolved + taps[tap] * padded[tap : tap + length].astype(f32)
         inner = jax.nn.silu(convolved)
-        partial = jnp.dot(inner.astype(bf16), projection, preferred_element_type=f32).astype(bf16)
-        projected = scatter_sum(partial, (rows, columns + extra), row_block(rows), "seq", 4)
-        maps = projected[:, rank:columns]
-        coarse = maps.astype(bf16)
-        fine = (maps - coarse.astype(f32)).astype(bf16)
-        sent = jnp.concatenate([projected[:, :rank].astype(bf16), coarse, fine], 1)
-        sent = jnp.pad(sent, ((0, 0), (0, -sent.shape[1] % LANES)))
-        everyone = exchange(sent, (length, sent.shape[1]), whole, row_block(rows), "seq", 5)
-        maps = everyone[:, rank:columns].astype(f32) + everyone[
-            :, columns : columns + 2 * nstate
-        ].astype(f32)
-        bc = maps.reshape(length // ROWS, ROWS, 2 * nstate).transpose(0, 2, 1)
+        partial = lax.dot_general(
+            input_projection[0],
+            inner.astype(bf16),
+            (((0,), (1,)), ((), ())),
+            preferred_element_type=f32,
+        ).astype(bf16)
+        everyone = project(partial, rank, rows, "seq", 4)
+        bc = everyone[rank:columns].astype(f32) + everyone[columns:].astype(f32)
         step_size = jax.nn.softplus(
-            jnp.dot(everyone[:, :rank], step_size_projection[0], preferred_element_type=f32)
+            lax.dot_general(
+                everyone[:rank],
+                step_size_projection[0],
+                (((0,), (0,)), ((), ())),
+                preferred_element_type=f32,
+            )
             + dt_bias
         )
         scanned = selective_scan(step_size, inner, bc, rates)
@@ -289,7 +428,12 @@
         if not last:
             moved = passed_along(mixed, "section")
             moved_ids = passed_along(all_ids[step], "section")
-        full = exchange(picked, (slots, model), whole, column_block(width), "seq", 6)
+        full = gather(picked, (slots, model), column_block(width), "seq", 6)
+        if last:
+            mixed = lax.all_to_all(
+                mixed.reshape(n, rows, width), "seq", split_axis=0, concat_axis=0
+            )
+            mixed = mixed.transpose(1, 0, 2).reshape(rows, model)
         full_float = full.astype(f32)
         moe_in = (
             full_float
@@ -313,8 +457,19 @@
         up_part = jnp.dot(moe_in, up_weight[0], preferred_element_type=f32)
         hidden = (jax.nn.silu(gate_part) * up_part).astype(bf16)
         terms = jnp.dot(hidden, down_weight[0], preferred_element_type=f32).astype(bf16)
-        expert_out = scatter_sum(terms, (slots, width), column_block(width), "seq", 7).astype(bf16)
-        new_rows = (picked.astype(f32) + route[:, None] * expert_out.astype(f32)).astype(bf16)
+        if last:
+            terms = terms.reshape(n, capacity, model)
+            expert_out = scatter_sum(terms, (capacity, model), slot_of, "seq", 8)
+            dispatch = lax.dynamic_slice(
+                dispatch, (me * capacity, me * rows), (capacity, rows)
+            )
+            routed = lax.dynamic_slice_in_dim(routed, me * rows, rows, 0)
+            route = lax.dynamic_slice_in_dim(route, me * capacity, capacity, 0)
+            picked = lax.dynamic_slice_in_dim(full, me * capacity, capacity, 0)
+        else:
+            expert_out = scatter_sum(terms, (slots, width), column_block(width), "seq", 7)
+        expert_out = expert_out.astype(bf16).astype(f32)
+        new_rows = (picked.astype(f32) + route[:, None] * expert_out).astype(bf16)
         if not last:
             new_rows = passed_along(new_rows, "section")
             dispatch, routed = dispatch_of(moved_ids, n, capacity)
@@ -323,8 +478,7 @@
             dispatch, new_rows, (((0,), (0,)), ((), ())), preferred_element_type=f32
         ).astype(bf16)
         present = jnp.where(routed[:, None], placed, mixed)
-    produced = exchange(present, (rows, model), row_block(rows), column_block(width), "seq", 8)
-    return produced[None]
+    return present[None]
 
 
 def solution(mesh):

time: 281 us -> 212 us (0.75)
  Pallas kernels: 173 us -> 143 us
  matrix products: 59.4 us -> 40.7 us
  other arithmetic: 25.9 us -> 11.6 us
  local copies, waits for them, and re-layouts: 13.1 us -> 3.85 us
  starting transfers between devices: 4.23 us -> 8.24 us
    pallas_call x4 -> x2, Pallas kernels: 46.1 us -> 18.6 us  [scatter_sum(): pl.pallas_call(functools.partial(scatter_sum_kernel, axis, src_at), out_s...]
    pallas_call x8 -> x6, Pallas kernels: 85.3 us -> 71.1 us  [the longest x2 34 us: project(): pl.pallas_call(functools.partial(project_kernel, axis, column_block(block...]
    pallas_call x2, Pallas kernels: 41.8 us -> 53.1 us  [selective_scan(): pl.pallas_call(functools.partial(scan_kernel, nstate), out_shape=jax.Shap...]
    dot_general x2, matrix products: 14.3 us -> 4.71 us  [body(): gate_part = jnp.dot(moe_in, gate_weight[0], preferred_element_type=f32)]
    dot_general x4, matrix products: 9.59 us -> 3.77 us  [the longest x2 2.72 us: body(): lax.dot_general(everyone[:rank], step_size_projection[0], (((0,), (0,)),...]
    reshape x3 -> x1, local copies, waits for them, and re-layouts: 3.9 us -> 0.11 us  [body(): mixed = mixed.transpose(1, 0, 2).reshape(rows, model)]
    all_to_all x0 -> x1, starting transfers between devices: none -> 3.78 us  [body(): lax.all_to_all(mixed.reshape(n, rows, width), 'seq', split_axis=0, concat...]
    unnamed x38 -> x24, local copies, waits for them, and re-layouts: 5.07 us -> 1.29 us
  transfers between devices with their start and end apart: 3 -> 4, of which waited for: 1 -> 1; matrix products, arithmetic and copies ran while one was open for 9% -> 14% of each run, Pallas kernels for 7% -> 13%
where the time goes in v2:
time: 212 us
  Pallas kernels  143 us (67%)
  matrix products  40.7 us (19%)
  other arithmetic  11.6 us (5%)
  starting transfers between devices  8.24 us (4%)
  waiting for transfers between devices  4.23 us (2%)
  local copies, waits for them, and re-layouts  3.85 us (2%)
    pallas_call x2, Pallas kernels, selective_scan(): pl.pallas_call(functools.partial(scan_kernel, nstate), out_shape=jax.Shap...  53.1 us
    pallas_call x2, Pallas kernels, project(): pl.pallas_call(functools.partial(project_kernel, axis, column_block(block...  34 us
    dot_general x2, matrix products, body(): jnp.dot(hidden, down_weight[0], preferred_element_type=f32).astype(bf16)  25.5 us
    pallas_call x2, Pallas kernels, exchange(): pl.pallas_call(functools.partial(exchange_kernel, axis, parts), out_shape...  21.5 us
    pallas_call x2, Pallas kernels, scatter_sum(): pl.pallas_call(functools.partial(scatter_sum_kernel, axis, src_at), out_s...  18.6 us
    pallas_call x2, Pallas kernels, gather(): pl.pallas_call(functools.partial(gather_kernel, axis, place), out_shape=j...  15.6 us
    dot_general x2, matrix products, body(): gate_part = jnp.dot(moe_in, gate_weight[0], preferred_element_type=f32)  4.71 us
    ppermute x3, starting transfers between devices, passed_along(): return lax.ppermute(x, axis, [(i, (i + 1) % length) for i in range(length)])  4.46 us
  transfers between devices with their start and end apart: 4, of which 1 were waited for; matrix products, arithmetic and copies ran while one was open for 14% of the time, Pallas kernels for 13%

profile of v2, /device:TPU:1, one launch (start us, length us, event | category | flops | bytes accessed | tf_op | source)
XLA Modules:
  0.0 211.9 jit_solution(1987386147563754772)
XLA Ops:
  0.0 0.7 convert_element_type.202
  0.7 1.5 multiply_reduce_fusion
  2.3 1.2 copy-done.2
  3.5 16.7 %exchange_1.1 = (f32[8,8,128]{2,1,0:T(8,128)S(1)}, bf16[1024,512]{1,0:T(8,128)(2,1)S(1)}) custom-call(f32[8,128]{1,0:T(8,128)S(1)} %select_maximum_fusion.refs_0_, bf16[128,4096]{1,0:T(8,128)(2,1)S(1)} %bitcast.165), custom_call_target="tpu_custom_call" | custom-call | tf_op jit(solution)/shard_map/exchange_1/pallas_call | solution.py:59
  20.2 0.7 constant_dynamic-slice_fusion.3
  20.9 0.7 constant_dynamic-slice_fusion.4
  21.6 0.3 fusion.36
  22.0 0.9 constant_dynamic-slice_fusion.2
  22.9 1.4 divide_multiply_fusion.1.x_ref
  24.3 0.0 copy-start.4
  24.3 0.5 fusion.42.x_ref
  24.8 16.8 %project_4.2 = bf16[320,1024]{1,0:T(8,128)(2,1)S(1)} custom-call(bf16[288,1024]{1,0:T(8,128)(2,1)S(1)} %fusion.42.x_ref), custom_call_target="tpu_custom_call" | custom-call | tf_op jit(solution)/shard_map/project_4/pallas_call | solution.py:201
  41.7 0.8 multiply_bitcast_fusion.a_ref
  42.5 1.4 compare_select_fusion.1.dt_ref
  43.8 0.0 slice-start
  43.8 0.0 slice-start.1
  43.9 26.6 %selective_scan.2 = f32[1024,512]{1,0:T(8,128)S(1)} custom-call(f32[1024,512]{1,0:T(8,128)S(1)} %compare_select_fusion.1.dt_ref, f32[1024,512]{1,0:T(8,128)S(1)} %divide_multiply_fusion.1.x_ref, f32[32,1024]{1,0:T(8,128)S(1)} %convert_add_fusion.3.bc_ref, f32[16,512]{1,0:T(8,128)S(1)} %multiply_bitcast_fusion.a_ref), custom_call_target="tpu_custom_call" | custom-call | flops 50331648 | bytes 6291456 | tf_op jit(solution)/shard_map/selective_scan/pallas_call | solution.py:293
  70.4 0.0 slice-start.2
  70.4 1.7 fusion.37
  72.1 0.0 copy-start.3
  72.1 1.3 collective-permute-start.2
  73.5 1.5 collective-permute-start
  75.1 0.2 fusion.49
  75.3 0.3 convolution_convert_fusion.5.x_ref
  75.6 0.2 fusion.84
  75.8 8.4 %gather_6.2 = bf16[64,4096]{1,0:T(8,128)(2,1)S(1)} custom-call(bf16[64,512]{1,0:T(8,128)(2,1)S(1)} %convolution_convert_fusion.5.x_ref), custom_call_target="tpu_custom_call" | custom-call | tf_op jit(solution)/shard_map/gather_6/pallas_call | solution.py:122
  84.2 0.2 fusion.50
  84.5 0.2 fusion.47
  84.7 0.2 fusion.125
  84.9 0.0 slice-done.2
  84.9 2.4 %fusion.10 = f32[64,1536]{1,0:T(8,128)S(1)} fusion(bf16[1,4096,1536]{2,1,0:T(8,128)(2,1)S(1)} %bitcast.168, bf16[64,4096]{1,0:T(8,128)(2,1)S(1)} %gather_6.2, f32[4096]{0:T(1024)S(1)} %bitcast.173, f32[64]{0:T(128)S(1)} %add_rsqrt_fusion.2), kind=kOutput, calls=%fused_computation.10 | convolution fusion | flops 806354944 | bytes 13517056 | tf_op jit(solution)/shard_map/dot_general | solution.py:456
  87.2 0.0 copy-start.5
  87.3 12.8 %fusion.14.x_ref = bf16[64,4096]{1,0:T(8,128)(2,1)S(1)} fusion(bf16[1,1536,4096]{2,1,0:T(8,128)(2,1)} %param.28, bf16[1,4096,1536]{2,1,0:T(8,128)(2,1)} %param.27, f32[64,1536]{1,0:T(8,128)S(1)} %fusion.10, bf16[64,4096]{1,0:T(8,128)(2,1)S(1)} %gather_6.2, f32[4096]{0:T(1024)S(1)} %bitcast.174, f32[64]{0:T(128)S(1)} %add_rsqrt_fusion.2), kind=kOutput, calls=%fused_computation.17 | convolution fusion | flops 1612513280 | bytes 26624256 | tf_op jit(solution)/shard_map/dot_general | solution.py:459
  100.0 9.1 %scatter_sum_7.1 = f32[64,512]{1,0:T(8,128)S(1)} custom-call(bf16[64,4096]{1,0:T(8,128)(2,1)S(1)} %fusion.14.x_ref), custom_call_target="tpu_custom_call" | custom-call | tf_op jit(solution)/shard_map/scatter_sum_7/pallas_call | solution.py:175
  109.1 0.1 compare_convert_fusion
  109.2 0.3 fusion.119
  109.6 0.1 add_convert_fusion.1
  109.7 1.6 collective-permute-start.1
  111.3 0.0 collective-permute-done
  111.3 0.2 fusion.48
  111.5 4.2 %collective-permute-done.1 = bf16[64,512]{1,0:T(8,128)(2,1)S(1)} collective-permute-done((bf16[64,512]{1,0:T(8,128)(2,1)S(1)}, bf16[64,512]{1,0:T(8,128)(2,1)S(1)}, u32[]{:S(2)}, u32[]{:S(2)}) %collective-permute-start.1) | collective-permute-done | bytes 65568 | tf_op jit(solution)/shard_map/ppermute | solution.py:317
  115.8 0.0 collective-permute-done.2
  115.8 1.9 fusion.38
  117.7 4.8 %exchange_3.1 = f32[8,8,128]{2,1,0:T(8,128)S(1)} custom-call(f32[8,128]{1,0:T(8,128)S(1)} %bitcast.166), custom_call_target="tpu_custom_call" | custom-call | tf_op jit(solution)/shard_map/exchange_3/pallas_call | solution.py:59
  122.6 0.3 fusion.40
  122.9 1.4 divide_multiply_fusion.x_ref
  124.2 0.5 fusion.43.x_ref
  124.8 17.1 %project_4.3 = bf16[320,1024]{1,0:T(8,128)(2,1)S(1)} custom-call(bf16[288,1024]{1,0:T(8,128)(2,1)S(1)} %fusion.43.x_ref), custom_call_target="tpu_custom_call" | custom-call | tf_op jit(solution)/shard_map/project_4/pallas_call | solution.py:201
  141.9 0.0 slice-start.3
  141.9 1.4 compare_select_fusion.dt_ref
  143.3 0.0 slice-start.4
  143.3 26.6 %selective_scan.3 = f32[1024,512]{1,0:T(8,128)S(1)} custom-call(f32[1024,512]{1,0:T(8,128)S(1)} %compare_select_fusion.dt_ref, f32[1024,512]{1,0:T(8,128)S(1)} %divide_multiply_fusion.x_ref, f32[32,1024]{1,0:T(8,128)S(1)} %convert_add_fusion.2.bc_ref, f32[16,512]{1,0:T(8,128)S(1)} %multiply_bitcast_fusion.a_ref), custom_call_target="tpu_custom_call" | custom-call | flops 50331648 | bytes 6291456 | tf_op jit(solution)/shard_map/selective_scan/pallas_call | solution.py:293
  169.9 2.6 %fusion.41 = bf16[1024,512]{1,0:T(8,128)(2,1)} fusion(bf16[1024,512]{1,0:T(8,128)(2,1)S(1)} %get-tuple-element.24, f32[1024,512]{1,0:T(8,128)S(1)} %selective_scan.3, f32[512]{0:T(512)S(1)} %bitcast.203, bf16[1024,512]{1,0:T(8,128)(2,1)S(1)} %fusion.40, f32[512]{0:T(512)S(1)} %bitcast.201, f32[512]{0:T(512)S(1)} %bitcast.193, f32[512]{0:T(512)S(1)} %bitcast.197, ...), kind=kLoop, calls=%fused_computation.35 | loop fusion | flops 11010048 | bytes 5255168 | tf_op jit(solution)/shard_map/convert_element_type | solution.py:424
  172.6 1.5 convolution_convert_fusion.4.x_ref
  174.1 7.2 %gather_6.3 = bf16[64,4096]{1,0:T(8,128)(2,1)S(1)} custom-call(bf16[64,512]{1,0:T(8,128)(2,1)S(1)} %convolution_convert_fusion.4.x_ref), custom_call_target="tpu_custom_call" | custom-call | tf_op jit(solution)/shard_map/gather_6/pallas_call | solution.py:122
  181.2 0.2 fusion.53
  181.5 2.4 %fusion.8 = f32[64,1536]{1,0:T(8,128)S(1)} fusion(bf16[1,4096,1536]{2,1,0:T(8,128)(2,1)S(1)} %bitcast.170, bf16[64,4096]{1,0:T(8,128)(2,1)S(1)} %gather_6.3, f32[64]{0:T(128)S(1)} %add_rsqrt_fusion.1, f32[4096]{0:T(1024)S(1)} %bitcast.176), kind=kOutput, calls=%fused_computation.8 | convolution fusion | flops 806354944 | bytes 13517056 | tf_op jit(solution)/shard_map/dot_general | solution.py:456
  183.8 3.8 %all-to-all-start = ((bf16[8,128,512]{2,1,0:T(8,128)(2,1)}), bf16[8,128,512]{2,1,0:T(8,128)(2,1)S(1)}, u32[]{:S(2)}, u32[]{:S(2)}) async-start(bf16[8,128,512]{2,1,0:T(8,128)(2,1)} %bitcast.46), calls=%async_computation | async-start | bytes 2097152 | tf_op jit(solution)/shard_map/all_to_all | solution.py:433
  187.6 12.7 %fusion.20.x_ref = bf16[8,8,4096]{2,1,0:T(8,128)(2,1)S(1)} fusion(bf16[1,1536,4096]{2,1,0:T(8,128)(2,1)} %param.28, bf16[1,4096,1536]{2,1,0:T(8,128)(2,1)} %param.27, f32[64,1536]{1,0:T(8,128)S(1)} %fusion.8, bf16[64,4096]{1,0:T(8,128)(2,1)S(1)} %gather_6.3, f32[64]{0:T(128)S(1)} %add_rsqrt_fusion.1, f32[4096]{0:T(1024)S(1)} %bitcast.177), kind=kOutput, calls=%fused_computation.19 | convolution fusion | flops 1612513280 | bytes 26624256 | tf_op jit(solution)/shard_map/dot_general | solution.py:459
  200.3 9.5 %scatter_sum_8.1 = f32[8,4096]{1,0:T(8,128)S(1)} custom-call(bf16[8,8,4096]{2,1,0:T(8,128)(2,1)S(1)} %fusion.20.x_ref), custom_call_target="tpu_custom_call" | custom-call | tf_op jit(solution)/shard_map/scatter_sum_8/pallas_call | solution.py:175
  209.8 0.3 fusion.115
  210.2 0.1 dynamic_slice.42
  210.3 0.1 copy.17
  210.4 1.5 fusion.13
  (36 shorter events, 0.3 us)
Async XLA Ops:
  0.0 24.3 %copy-start = (bf16[1,512,288]{1,2,0:T(8,128)(2,1)S(1)}, bf16[1,512,288]{1,2,0:T(8,128)(2,1)}, u32[]{:S(2)}) copy-start(bf16[1,512,288]{1,2,0:T(8,128)(2,1)} %param.19) | copy-start | bytes 884740
  2.3 1.2 copy-start.2
  24.3 18.2 %copy-start.4 = (bf16[1,256,512]{2,1,0:T(8,128)(2,1)S(1)}, bf16[1,256,512]{2,1,0:T(8,128)(2,1)}, u32[]{:S(2)}) copy-start(bf16[1,256,512]{2,1,0:T(8,128)(2,1)} %param.20) | copy-start | bytes 786436
  43.8 41.0 %slice-start = ((s8[12582912]{0:T(1024)(128)(4,1)}), s8[4194304]{0:T(1024)(128)(4,1)S(1)}, s32[]{:S(2)}) async-start(s8[12582912]{0:T(1024)(128)(4,1)} %bitcast.167), calls=%async_computation.1 | async-start | bytes 8388608
  43.8 41.0 %slice-start.1 = ((s8[12582912]{0:T(1024)(128)(4,1)}), s8[4194304]{0:T(1024)(128)(4,1)S(1)}, s32[]{:S(2)}) async-start(s8[12582912]{0:T(1024)(128)(4,1)} %bitcast.167), calls=%async_computation.2 | async-start | bytes 8388608
  70.4 14.4 %slice-start.2 = ((s8[12582912]{0:T(1024)(128)(4,1)}), s8[4194304]{0:T(1024)(128)(4,1)S(1)}, s32[]{:S(2)}) async-start(s8[12582912]{0:T(1024)(128)(4,1)} %bitcast.167), calls=%async_computation.3 | async-start | bytes 8388608
  72.1 12.7 %copy-start.3 = (f32[1,4096]{1,0:T(1,128)S(1)}, f32[1,4096]{1,0:T(1,128)}, u32[]{:S(2)}) copy-start(f32[1,4096]{1,0:T(1,128)} %param.24) | copy-start | bytes 49156
  72.1 43.6 %collective-permute-start.2 = (bf16[1024,512]{1,0:T(8,128)(2,1)S(1)}, bf16[1024,512]{1,0:T(8,128)(2,1)}, u32[]{:S(2)}, u32[]{:S(2)}) collective-permute-start(bf16[1024,512]{1,0:T(8,128)(2,1)S(1)} %fusion.37), channel_id=1, source_target_pairs={{0,8},{8,16},{16,24},{24,0},{1,9},{9,17},{17,25},{25,1},{2,10},{10... | collective-permute-start | bytes 3145736 | tf_op jit(solution)/shard_map/ppermute | solution.py:317
  73.5 37.8 %collective-permute-start = (f32[1024,2]{0,1:T(2,128)S(1)}, f32[1024,2]{0,1:T(2,128)S(1)}, u32[]{:S(2)}, u32[]{:S(2)}) collective-permute-start(f32[1024,2]{0,1:T(2,128)S(1)} %get-tuple-element.20), channel_id=1, source_target_pairs={{0,8},{8,16},{16,24},{24,0},{1,9},{9,17},{17,25},{25,1},{2,10},{10... | collective-permute-start | bytes 24584 | tf_op jit(solution)/shard_map/ppermute | solution.py:317
  87.2 22.0 %copy-start.5 = (bf16[1,4096,16]{1,2,0:T(8,128)(2,1)S(1)}, bf16[1,4096,16]{1,2,0:T(8,128)(2,1)}, u32[]{:S(2)}) copy-start(bf16[1,4096,16]{1,2,0:T(8,128)(2,1)} %param.25) | copy-start | bytes 393220
  109.7 6.1 %collective-permute-start.1 = (bf16[64,512]{1,0:T(8,128)(2,1)S(1)}, bf16[64,512]{1,0:T(8,128)(2,1)S(1)}, u32[]{:S(2)}, u32[]{:S(2)}) collective-permute-start(bf16[64,512]{1,0:T(8,128)(2,1)S(1)} %add_convert_fusion.1), channel_id=1, source_target_pairs={{0,8},{8,16},{16,24},{24,0},{1,9},{9,17},{17,25},{25,1},{2,10},{10... | collective-permute-start | bytes 196616 | tf_op jit(solution)/shard_map/ppermute | solution.py:317
  141.9 39.5 %slice-start.3 = ((s8[12582912]{0:T(1024)(128)(4,1)}), s8[4194304]{0:T(1024)(128)(4,1)S(1)}, s32[]{:S(2)}) async-start(s8[12582912]{0:T(1024)(128)(4,1)} %bitcast.169), calls=%async_computation.4 | async-start | bytes 8388608
  143.3 38.1 %slice-start.4 = ((s8[12582912]{0:T(1024)(128)(4,1)}), s8[4194304]{0:T(1024)(128)(4,1)S(1)}, s32[]{:S(2)}) async-start(s8[12582912]{0:T(1024)(128)(4,1)} %bitcast.169), calls=%async_computation.5 | async-start | bytes 8388608
  143.3 38.1 %slice-start.5 = ((s8[12582912]{0:T(1024)(128)(4,1)}), s8[4194304]{0:T(1024)(128)(4,1)S(1)}, s32[]{:S(2)}) async-start(s8[12582912]{0:T(1024)(128)(4,1)} %bitcast.169), calls=%async_computation.6 | async-start | bytes 8388608
  183.8 26.5 %all-to-all-start = ((bf16[8,128,512]{2,1,0:T(8,128)(2,1)}), bf16[8,128,512]{2,1,0:T(8,128)(2,1)S(1)}, u32[]{:S(2)}, u32[]{:S(2)}) async-start(bf16[8,128,512]{2,1,0:T(8,128)(2,1)} %bitcast.46), calls=%async_computation | async-start | bytes 2097152 | tf_op jit(solution)/shard_map/all_to_all | solution.py:433
  210.3 1.6 copy-start.1
